TPU v7x, 32 devices: a whole 2x2x4 slice. The times are simulated.
32 devices in a mesh: gx: 8 (over z, core), gy: 4 (over y, x).
Axes of the slice: x: 2, y: 2, z: 4, core: 2. Of those that a mesh axis runs over, the one named last changes fastest.
Arguments:
- rhs_field: float32 [128, 64, 128], P('gx', 'gy'), may hold values from -10 to 10
- diag_blocks: bfloat16 [128, 64, 128, 128], P('gx', 'gy'), may hold values from -1 to 4, as said below
- face_lift: bfloat16 [4, 128, 128], replicated, may hold values from -0.5 to 0.5
- face_state: int32 [128, 64, 4], P('gx', 'gy'), may hold values from 0 to 2
- restrict_basis: float32 [128, 8], replicated, may hold values from -0.5 to 0.5
- coarse_inverse: float32 [128, 64, 8, 8], P('gx', 'gy'), may hold values from -0.4 to 1.2
Outputs:
- solution_field: float32 [128, 64, 128], P('gx', 'gy')
- hessenberg: float32 [3, 2], replicated
Inputs may be any that keep to these rules, and one draw needn't show every extreme that they name: `diag_blocks`: each block has diagonal entries between 2 and 4 and small off-diagonal entries.
All inputs are finite; a program needn't handle non-finite values.
Results may differ from a plain program's by a relative error of at most 0.0023.
Values may be sent and summed in bfloat16 or wider, within the bound.
A program may use at most 64 MiB of HBM per device.

v0:
```python
import functools
import jax
import jax.numpy as jnp
from jax import lax
from jax.experimental import pallas as pl
from jax.experimental.pallas import tpu as pltpu
from jax.sharding import PartitionSpec as P

MESH = pl.DeviceIdType.MESH
F32 = jnp.float32
BF16 = jnp.bfloat16


def hdot(a, b, dims=(((1,), (0,)), ((), ()))):
    return lax.dot_general(a, b, dims, precision=lax.Precision.HIGHEST, preferred_element_type=F32)


def total(x):
    return jnp.sum(jnp.sum(x, axis=0, keepdims=True), axis=1, keepdims=True)


def safe_div(a, b):
    return jnp.where(b > 0, a / jnp.where(b > 0, b, 1.0), 0.0)


def iota(shape, dim):
    return lax.broadcasted_iota(jnp.int32, shape, dim)


def kernel(nx, ny, ti, tj, n, kc, rhs_h, diag, lift_h, state_h, basis_h, cinv_h, out, hess_out,
           rhs, lift, state, basis, cinv,
           dvm, wts, masks, cext, wbuf, sends, halos, csend, chalo, sums, msgs,
           isem, dsem, ssem, rsem, lsend, lrecv, msend, mrecv, know):
    gx = lax.axis_index("gx")
    gy = lax.axis_index("gy")
    me = gx * ny + gy
    count = nx * ny
    elems = ti * tj
    kk = kc * kc

    loads = [pltpu.make_async_copy(a, b, isem.at[q]) for q, (a, b) in enumerate(
        ((rhs_h, rhs), (basis_h, basis), (cinv_h, cinv), (state_h, state), (lift_h, lift)))]
    for c in loads:
        c.start()
    dcopies = [pltpu.make_async_copy(diag.at[q], dvm.at[q], dsem.at[q]) for q in range(ti)]
    for c in dcopies:
        c.start()

    barrier = pltpu.get_barrier_semaphore()

    has_n, has_s, has_w, has_e = gx > 0, gx < nx - 1, gy > 0, gy < ny - 1
    n_i, s_i, w_i, e_i = [v.astype(jnp.int32) for v in (has_n, has_s, has_w, has_e)]
    near = [(has_n, -1, k) for k in range(ny)] + [(has_s, 1, k) for k in range(ny)] + [
        (None, 0, k) for k in range(1, ny)]
    near_count = ny - 1 + ny * (n_i + s_i)

    def when(ok, run):
        if ok is None:
            run()
        else:
            pl.when(ok)(run)

    sums[...] = jnp.zeros_like(sums)
    for ok, d, k in near:
        def hello(d=d, k=k):
            pl.semaphore_signal(barrier, inc=1, device_id=(gx + d, lax.rem(gy + k, ny)), device_id_type=MESH)
        when(ok, hello)

    steps = []
    r = 2
    while r < nx - 1:
        steps.append(r)
        r *= 2

    def tell(q):
        r = steps[q]
        for ok, d in ((gx >= r, -r), (gx + r < nx, r)):
            def one(d=d):
                pl.semaphore_signal(know.at[q], inc=1, device_id=(gx + d, gy), device_id_type=MESH)
            when(ok, one)

    def learn(q):
        r = steps[q]
        amount = (gx >= r).astype(jnp.int32) + (gx + r < nx).astype(jnp.int32)
        pl.semaphore_wait(know.at[q], amount)

    def line_copy(g, d, k):
        return pltpu.make_async_remote_copy(
            src_ref=sums.at[g, ny + gy], dst_ref=sums.at[g, (1 - d) * ny + gy],
            send_sem=lsend.at[g, d + 1], recv_sem=lrecv.at[g, 1 - d],
            device_id=(gx + d, lax.rem(gy + k, ny)), device_id_type=MESH)

    def share_lines(g):
        for ok, d, k in near:
            when(ok, lambda d=d, k=k: line_copy(g, d, k).start())

    def line_wait(g, which):
        for ok, d in ((has_n, -1), (has_s, 1), (None, 0)):
            def one(d=d):
                part = sums.at[g, pl.ds((d + 1) * ny, ny if d else ny - 1)]
                c = pltpu.make_async_remote_copy(
                    src_ref=part, dst_ref=part, send_sem=lsend.at[g, d + 1], recv_sem=lrecv.at[g, d + 1],
                    device_id=(gx, gy), device_id_type=MESH)
                if which == "send":
                    c.wait_send()
                else:
                    c.wait_recv()
            when(ok, one)

    h = 2 * ti + 2 * tj
    o_n, o_s, o_w, o_e = 0, tj, 2 * tj, 2 * tj + 2 * ti
    o_nw = 2 * tj + 4 * ti
    o_ne, o_sw, o_se = o_nw + 8, o_nw + 16, o_nw + 24
    hrows = o_nw + 32
    routes = [
        (has_n, (gx - 1, gy), o_n, o_s, tj),
        (has_s, (gx + 1, gy), o_s, o_n, tj),
        (has_w, (gx, gy - 1), o_w, o_e, 2 * ti),
        (has_e, (gx, gy + 1), o_e, o_w, 2 * ti),
        (jnp.logical_and(has_n, has_w), (gx - 1, gy - 1), o_nw, o_se, 8),
        (jnp.logical_and(has_n, has_e), (gx - 1, gy + 1), o_ne, o_sw, 8),
        (jnp.logical_and(has_s, has_w), (gx + 1, gy - 1), o_sw, o_ne, 8),
        (jnp.logical_and(has_s, has_e), (gx + 1, gy + 1), o_se, o_nw, 8),
    ]
    croutes = [
        (has_n, (gx - 1, gy), 0, tj, tj),
        (has_s, (gx + 1, gy), tj, 0, tj),
        (has_w, (gx, gy - 1), 2 * tj, 2 * tj + ti, ti),
        (has_e, (gx, gy + 1), 2 * tj + ti, 2 * tj, ti),
    ]
    opposite = [1, 0, 3, 2, 7, 6, 5, 4]

    def rim_copies(g):
        return [(ok, pltpu.make_async_remote_copy(
            src_ref=sends.at[g, pl.ds(src, rows)], dst_ref=halos.at[g, pl.ds(dst, rows)],
            send_sem=ssem.at[g, d], recv_sem=rsem.at[g, opposite[d]],
            device_id=dev, device_id_type=MESH)) for d, (ok, dev, src, dst, rows) in enumerate(routes)]

    def coarse_copies():
        return [(ok, pltpu.make_async_remote_copy(
            src_ref=csend.at[pl.ds(src, rows)], dst_ref=chalo.at[pl.ds(dst, rows)],
            send_sem=ssem.at[2, d], recv_sem=rsem.at[2, opposite[d]],
            device_id=dev, device_id_type=MESH)) for d, (ok, dev, src, dst, rows) in enumerate(croutes)]

    def rim_wait(g, which):
        table = routes if g < 2 else croutes
        for d, (ok, dev, src, dst, rows) in enumerate(table):
            @pl.when(ok)
            def _(d=d, dev=dev, src=src, rows=rows):
                if g < 2:
                    s, r = sends.at[g, pl.ds(src, rows)], halos.at[g, pl.ds(src, rows)]
                else:
                    s, r = csend.at[pl.ds(src, rows)], chalo.at[pl.ds(src, rows)]
                c = pltpu.make_async_remote_copy(
                    src_ref=s, dst_ref=r, send_sem=ssem.at[g, d], recv_sem=rsem.at[g, d],
                    device_id=dev, device_id_type=MESH)
                if which == "send":
                    c.wait_send()
                else:
                    c.wait_recv()

    def start_all(copies):
        for ok, c in copies:
            @pl.when(ok)
            def _(c=c):
                c.start()

    def broadcast():
        def one(k, carry):
            t = lax.rem(me + k, count)
            pltpu.make_async_remote_copy(
                src_ref=msgs.at[me], dst_ref=msgs.at[me], send_sem=msend.at[0], recv_sem=mrecv.at[0],
                device_id=(t // ny, lax.rem(t, ny)), device_id_type=MESH).start()
            return carry
        lax.fori_loop(1, count, one, 0)

    def bc_wait(which):
        part = msgs.at[pl.ds(0, count - 1)]
        c = pltpu.make_async_remote_copy(
            src_ref=part, dst_ref=part, send_sem=msend.at[0], recv_sem=mrecv.at[0],
            device_id=(gx, gy), device_id_type=MESH)
        if which == "send":
            c.wait_send()
        else:
            c.wait_recv()

    def fill_sends(g, ref):
        sends[g, o_n:o_n + tj] = ref[0]
        sends[g, o_s:o_s + tj] = ref[ti - 1]
        sends[g, o_w:o_w + ti] = ref[:, 0, :]
        sends[g, o_w + ti:o_w + 2 * ti] = ref[:, 1, :]
        sends[g, o_e:o_e + ti] = ref[:, tj - 1, :]
        sends[g, o_e + ti:o_e + 2 * ti] = ref[:, tj - 2, :]
        sends[g, o_nw:o_nw + 8] = jnp.broadcast_to(ref[0, 0:1, :], (8, n))
        sends[g, o_ne:o_ne + 8] = jnp.broadcast_to(ref[0, tj - 1:tj, :], (8, n))
        sends[g, o_sw:o_sw + 8] = jnp.broadcast_to(ref[ti - 1, 0:1, :], (8, n))
        sends[g, o_se:o_se + 8] = jnp.broadcast_to(ref[ti - 1, tj - 1:tj, :], (8, n))

    lane1 = iota((1, n), 1)

    def message(values):
        row = jnp.zeros((1, n), F32)
        for p, v in enumerate(values):
            row = jnp.where(lane1 == p, v, row)
        return row

    e1 = (iota((kc, n), 1) // kc == iota((kc, n), 0)).astype(F32)
    e3 = (lax.rem(iota((kc, n), 1), kc) == iota((kc, n), 0)).astype(F32)
    pick = iota((ti, n), 1) // kc == iota((ti, n), 0)
    loads[0].wait()
    loads[1].wait()
    Rt = basis[...]
    over_first = (((0,), (0,)), ((), ()))
    RT = hdot(Rt, e3, over_first)

    def packed_rowsum(f3):
        rows = hdot(jnp.sum(f3, axis=1), RT)
        return jnp.sum(jnp.where(pick, rows, 0.0), axis=0, keepdims=True)

    rhs3 = rhs[...]
    rhs2 = rhs3.reshape(elems, n)
    fill_sends(0, rhs)
    sums[0, ny + gy] = packed_rowsum(rhs3)

    pl.semaphore_wait(barrier, near_count)
    start_all(rim_copies(0))
    share_lines(0)
    loads[2].wait()
    cext[...] = jnp.zeros_like(cext)
    eye = (iota((tj, tj), 0) == iota((tj, tj), 1)).astype(F32)
    for q in range(ti):
        cext[q * tj:(q + 1) * tj, 0:kk] = hdot(eye, cinv[q], (((1,), (1,)), ((), ())))
    c3d = cext[0:elems].reshape(ti, tj, n)
    csend[0:tj] = c3d[0]
    csend[tj:2 * tj] = c3d[ti - 1]
    csend[2 * tj:2 * tj + ti] = c3d[:, 0, :]
    csend[2 * tj + ti:2 * tj + 2 * ti] = c3d[:, tj - 1, :]
    start_all(coarse_copies())

    RE = hdot(Rt, e1, over_first)
    e4 = (lax.rem(iota((n, kc), 0), kc) == iota((n, kc), 1)).astype(F32)
    RF = hdot(e4, Rt)
    G = (lax.rem(iota((n, n), 0), kc) == iota((n, n), 1) // kc).astype(F32)
    flip = (iota((n, n), 0) + iota((n, n), 1) == n - 1).astype(BF16)
    loads[4].wait()
    for f in range(4):
        wts[2 * f * n:(2 * f + 1) * n] = lift[f]
        wts[(2 * f + 1) * n:(2 * f + 2) * n] = jnp.dot(flip, lift[f], preferred_element_type=F32).astype(BF16)
    loads[3].wait()
    own_j = lax.rem(iota((elems, tj), 0), tj) == iota((elems, tj), 1)
    ones = jnp.ones((tj, n), BF16)
    for f in range(4):
        rows = state[:, f, :].astype(F32)
        wide = jnp.broadcast_to(rows[:, None, :], (ti, tj, tj)).reshape(elems, tj)
        col = jnp.dot(jnp.where(own_j, wide, 0.0).astype(BF16), ones, preferred_element_type=F32)
        masks[2 * f] = (col == 1.0).astype(F32)
        masks[2 * f + 1] = (col == 2.0).astype(F32)

    hrow = iota((hrows, 1), 0)
    valid = jnp.where(hrow < o_s, n_i, jnp.where(hrow < o_w, s_i, jnp.where(
        hrow < o_e, w_i, jnp.where(hrow < o_nw, e_i, jnp.where(
            hrow < o_ne, n_i * w_i, jnp.where(hrow < o_sw, n_i * e_i, jnp.where(
                hrow < o_se, s_i * w_i, s_i * e_i))))))) > 0

    jrow = lax.rem(iota((elems, 1), 0), tj)
    trow = iota((tj, 1), 0)

    def spread(col):
        return jnp.broadcast_to(col[:, None, :], (ti, tj, n)).reshape(elems, n)

    def left_of(x, edge):
        return jnp.where(jrow == 0, spread(edge), pltpu.roll(x, 1, 0))

    def right_of(x, edge):
        return jnp.where(jrow == tj - 1, spread(edge), pltpu.roll(x, elems - 1, 0))

    def line_sum(g, d):
        acc = sums[g, (d + 1) * ny]
        for q in range(1, ny):
            acc = acc + sums[g, (d + 1) * ny + q]
        return acc

    def three_lines(g):
        return line_sum(g, 0), line_sum(g, -1), line_sum(g, 1)

    def precondition(f_own, f_halo, lines, coarse):
        p_c, p_n, p_s = lines
        stack = jnp.concatenate([
            jnp.where(pick, jnp.broadcast_to(p_c, (ti, n)), 0.0),
            jnp.broadcast_to(jnp.where(lane1 // kc == ti - 1, p_n, 0.0), (8, n)),
            jnp.broadcast_to(jnp.where(lane1 // kc == 0, p_s, 0.0), (8, n))], axis=0)
        mean = hdot(stack, G) * (1.0 / (ny * tj))
        m_c, m_n, m_s = mean[0:ti], mean[ti:ti + 1], mean[ti + 8:ti + 9]
        c_own = coarse - spread(m_c)
        c_halo = hdot(f_halo, RE)
        m_halo = jnp.concatenate([
            jnp.broadcast_to(m_n, (tj, n)), jnp.broadcast_to(m_s, (tj, n)), m_c, m_c, m_c, m_c,
            jnp.broadcast_to(m_n, (16, n)), jnp.broadcast_to(m_s, (16, n))], axis=0)
        c_halo = jnp.where(valid, c_halo - m_halo, 0.0)
        c_w1, c_w2 = c_halo[o_w:o_w + ti], c_halo[o_w + ti:o_e]
        c_e1, c_e2 = c_halo[o_e:o_e + ti], c_halo[o_e + ti:o_nw]
        c_n, c_s = c_halo[o_n:o_n + tj], c_halo[o_s:o_s + tj]
        c3 = c_own.reshape(ti, tj, n)
        s_own = c_own + 0.25 * (left_of(c_own, c_w1) + right_of(c_own, c_e1))

        def row_smooth(x, lo, hi):
            left = jnp.where(trow == 0, lo, pltpu.roll(x, 1, 0))
            right = jnp.where(trow == tj - 1, hi, pltpu.roll(x, tj - 1, 0))
            return x + 0.25 * (left + right)
        s_n = row_smooth(c_n, c_halo[o_nw:o_nw + 1], c_halo[o_ne:o_ne + 1])
        s_s = row_smooth(c_s, c_halo[o_sw:o_sw + 1], c_halo[o_se:o_se + 1])
        s_w = c_w1 + 0.25 * (c_w2 + c3[:, 0, :])
        s_e = c_e1 + 0.25 * (c3[:, tj - 1, :] + c_e2)
        z_own = f_own + hdot(s_own * cext[0:elems], RF)
        f_rim = jnp.concatenate([f_halo[o_n:o_w], f_halo[o_w:o_w + ti], f_halo[o_e:o_e + ti]], axis=0)
        ok_rim = jnp.concatenate([valid[o_n:o_w], valid[o_w:o_w + ti], valid[o_e:o_e + ti]], axis=0)
        s_rim = jnp.concatenate([s_n, s_s, s_w, s_e], axis=0)
        z_rim = jnp.where(ok_rim, f_rim + hdot(s_rim * cext[elems:elems + h], RF), 0.0)
        return z_own, z_rim

    def operator(z, z_rim):
        nb = [
            jnp.concatenate([z_rim[0:tj], z[0:elems - tj]], axis=0),
            jnp.concatenate([z[tj:], z_rim[tj:2 * tj]], axis=0),
            left_of(z, z_rim[2 * tj:2 * tj + ti]),
            right_of(z, z_rim[2 * tj + ti:2 * tj + 2 * ti]),
        ]
        cols = []
        for f in range(4):
            cols.append((nb[f] * masks[2 * f]).astype(BF16))
            cols.append((nb[f] * masks[2 * f + 1]).astype(BF16))
        lifted = jnp.dot(jnp.concatenate(cols, axis=1), wts[...], preferred_element_type=F32)
        wbuf[...] = lifted.reshape(ti, tj, n)
        half = tj // 2
        for q in range(ti):
            a = z[q * tj:(q + 1) * tj]
            hi = a.astype(BF16)
            both = jnp.concatenate([hi, (a - hi.astype(F32)).astype(BF16)], axis=0)
            lhs = jnp.concatenate([both * keep[t] for t in range(half)], axis=1)
            rhs_w = jnp.concatenate(
                [dvm[q, 0:half].reshape(half * n, n), dvm[q, half:tj].reshape(half * n, n)], axis=1)
            prod = jnp.dot(lhs, rhs_w, preferred_element_type=F32)
            prod = prod[0:tj] + prod[tj:2 * tj]
            wbuf[q] += jnp.concatenate([prod[0:half, 0:n], prod[half:tj, n:2 * n]], axis=0)

    keep = [(lax.rem(iota((2 * tj, n), 0), tj // 2) == t).astype(F32).astype(BF16) for t in range(tj // 2)]
    coarse_rhs = hdot(rhs2, RE)
    line_wait(0, "recv")
    rim_wait(0, "recv")
    rim_wait(2, "recv")
    if steps:
        tell(0)

    cext[elems:elems + h] = chalo[...]
    z1, z1_rim = precondition(rhs2, jnp.where(valid, halos[0], 0.0), three_lines(0), coarse_rhs)
    for c in dcopies:
        c.wait()
    operator(z1, z1_rim)
    fill_sends(1, wbuf)
    start_all(rim_copies(1))
    sums[1, ny + gy] = packed_rowsum(wbuf[...])
    share_lines(1)
    w1 = wbuf[...].reshape(elems, n)
    for q in range(len(steps)):
        learn(q)
        if q + 1 < len(steps):
            tell(q + 1)
    own_n1 = total(rhs2 * rhs2)
    p_one = safe_div(total(rhs2 * w1), own_n1)
    gap = w1 - p_one * rhs2
    own_n2 = total(gap * gap)
    coarse_w = hdot(w1, RE)
    line_wait(1, "recv")
    rim_wait(1, "recv")

    z2, z2_rim = precondition(w1, jnp.where(valid, halos[1], 0.0), three_lines(1), coarse_w)
    operator(z2, z2_rim)
    w2 = wbuf[...].reshape(elems, n)
    p_two = safe_div(total(rhs2 * w2), own_n1)
    q_two = safe_div(total(gap * w2), own_n2)
    rest = w2 - p_two * rhs2 - q_two * gap
    msgs[me] = message([own_n1, p_one, own_n2, p_two, q_two, total(rest * rest)])
    broadcast()
    bc_wait("recv")
    Y = msgs[:, 0, :]
    l_n1, l_p, l_n2, l_a, l_b, l_n3 = [Y[:, q:q + 1] for q in range(6)]

    def over(x):
        return jnp.sum(x, axis=0, keepdims=True)
    len2 = over(l_n1)
    start_len = jnp.sqrt(len2)
    h11 = over(l_p * l_n1) / len2
    dev = l_p - h11
    gap2 = over(dev * dev * l_n1 + l_n2)
    gap_len = jnp.sqrt(gap2)
    h21 = gap_len / start_len
    e_one = l_a - h11 * l_p
    e_two = l_b - h11
    t12 = over(e_one * l_n1) / len2
    h12 = t12 * start_len / gap_len
    h22 = over(dev * e_one * l_n1 + e_two * l_n2) / gap2
    g_one = e_one - t12 - h22 * dev
    g_two = e_two - h22
    h32 = jnp.sqrt(over(g_one * g_one * l_n1 + g_two * g_two * l_n2 + l_n3)) / gap_len

    first = jnp.sqrt(h11 * h11 + h21 * h21)
    cos_one = h11 / first
    sin_one = h21 / first
    upper = cos_one * h12 + sin_one * h22
    lower = -sin_one * h12 + cos_one * h22
    second = jnp.sqrt(lower * lower + h32 * h32)
    cos_two = lower / second
    y2 = cos_two * (-sin_one * start_len) / second
    y1 = (cos_one * start_len - upper * y2) / first
    c2 = y2 / gap_len
    c1 = y1 / start_len - c2 * h11
    out[...] = (c1 * z1 + c2 * z2).reshape(ti, tj, n)
    hr, hc = iota((2, 3), 1), iota((2, 3), 0)
    hess_out[...] = jnp.where(
        hr == 0, jnp.where(hc == 0, h11, h12),
        jnp.where(hr == 1, jnp.where(hc == 0, h21, h22), jnp.where(hc == 0, 0.0, h32)))

    bc_wait("send")
    for g in range(2):
        line_wait(g, "send")
    for g in range(3):
        rim_wait(g, "send")


def hand_on(sol_in, hess_in, sol_out, hess_out):
    sol_out[...] = sol_in[...]
    hess_out[...] = hess_in[...]


def solution(mesh):
    nx, ny = mesh.shape["gx"], mesh.shape["gy"]

    def body(rhs, diag, lift, state, basis, cinv):
        ti, tj, n = rhs.shape
        kc = basis.shape[1]
        cflat = jnp.transpose(cinv, (0, 2, 3, 1)).reshape(ti, kc * kc, tj)
        sflat = jnp.transpose(state, (0, 2, 1))
        hrows = 2 * tj + 4 * ti + 32
        h = 2 * ti + 2 * tj
        vm = pl.BlockSpec(memory_space=pltpu.VMEM)
        hbm = pl.BlockSpec(memory_space=pltpu.HBM)
        sol, hess = pl.pallas_call(
            functools.partial(kernel, nx, ny, ti, tj, n, kc),
            out_shape=(jax.ShapeDtypeStruct((ti, tj, n), F32), jax.ShapeDtypeStruct((2, 3), F32)),
            in_specs=[hbm] * 6,
            out_specs=(vm, vm),
            scratch_shapes=[
                pltpu.VMEM((ti, tj, n), F32),
                pltpu.VMEM((4, n, n), BF16),
                pltpu.VMEM((ti, 4, tj), jnp.int32),
                pltpu.VMEM((kc, n), F32),
                pltpu.VMEM((ti, kc * kc, tj), F32),
                pltpu.VMEM((ti, tj, n, n), BF16),
                pltpu.VMEM((8 * n, n), BF16),
                pltpu.VMEM((8, ti * tj, n), F32),
                pltpu.VMEM((ti * tj + h, n), F32),
                pltpu.VMEM((ti, tj, n), F32),
                pltpu.VMEM((2, hrows, n), F32),
                pltpu.VMEM((2, hrows, n), F32),
                pltpu.VMEM((h, n), F32),
                pltpu.VMEM((h, n), F32),
                pltpu.VMEM((2, 3 * ny, 1, n), F32),
                pltpu.VMEM((nx * ny, 1, n), F32),
                pltpu.SemaphoreType.DMA((5,)),
                pltpu.SemaphoreType.DMA((ti,)),
                pltpu.SemaphoreType.DMA((3, 8)),
                pltpu.SemaphoreType.DMA((3, 8)),
                pltpu.SemaphoreType.DMA((2, 3)),
                pltpu.SemaphoreType.DMA((2, 3)),
                pltpu.SemaphoreType.DMA((1,)),
                pltpu.SemaphoreType.DMA((1,)),
                pltpu.SemaphoreType.REGULAR((max(1, nx.bit_length()),)),
            ],
            compiler_params=pltpu.CompilerParams(collective_id=0, has_side_effects=True,
                                                 vmem_limit_bytes=60 * 1024 * 1024),
        )(rhs, diag, lift, sflat, basis.T, cflat)
        sol, hess = pl.pallas_call(
            hand_on,
            out_shape=(jax.ShapeDtypeStruct(sol.shape, F32), jax.ShapeDtypeStruct(hess.shape, F32)),
            in_specs=[vm, vm],
            out_specs=(vm, vm),
            compiler_params=pltpu.CompilerParams(vmem_limit_bytes=60 * 1024 * 1024),
        )(sol, hess)
        return sol, hess.T

    in_specs = (P("gx", "gy", None), P("gx", "gy", None, None), P(), P("gx", "gy", None), P(),
                P("gx", "gy", None, None))
    return jax.shard_map(body, mesh=mesh, in_specs=in_specs, out_specs=(P("gx", "gy", None), P()), check_vma=False)
```

profile of v0, /device:TPU:0, one launch (start us, length us, event | category | flops | bytes accessed | tf_op | source)
XLA Modules:
  0.0 26.9 jit_solution(4267767972876679488)
XLA Ops:
  0.6 24.7 %shard_map.77 = (f32[16,16,128]{2,1,0:T(8,128)}, f32[2,3]{1,0:T(2,128)}) custom-call(f32[16,16,128]{2,1,0:T(8,128)} %rhs_h.1, bf16[16,16,128,128]{3,2,1,0:T(8,128)(2,1)} %diag.1, bf16[4,128,128]{2,1,0:T(8,128)(2,1)} %lift_h.1, s32[16,4,16]{2,1,0:T(4,128)} %bitcast.7, f32[8,128]{1,0:T(8,128)} %bitcast.8, f32[16,64,16]{2,1,0:T(8,128)} %bitcast.6), custom_call_target="tpu_custom_call" | custom-call | tf_op jit(solution)/shard_map/pallas_call | solution.py:447
  25.3 1.6 %shard_map.78 = (f32[16,16,128]{2,1,0:T(8,128)}, f32[2,3]{1,0:T(2,128)}) custom-call(f32[16,16,128]{2,1,0:T(8,128)} %get-tuple-element.6.sol_in, f32[2,3]{1,0:T(2,128)} %get-tuple-element.7.hess_in), custom_call_target="tpu_custom_call" | custom-call | tf_op jit(solution)/shard_map/pallas_call | solution.py:482
where the time goes:
time: 27.1 us; the launch traced here: 26.9 us
  Pallas kernels  26.3 us (97%)
  between operations  0.64 us (2%)
    pallas_call x1, Pallas kernels, body(): pl.pallas_call(functools.partial(kernel, nx, ny, ti, tj, n, kc), out_shap...  24.7 us
    pallas_call x1, Pallas kernels, body(): pl.pallas_call(hand_on, out_shape=(jax.ShapeDtypeStruct(sol.shape, F32),...  1.57 us

commit v1 on v0

--- a/solution.py
+++ b/solution.py
@@ -477,14 +477,14 @@
                 pltpu.SemaphoreType.REGULAR((max(1, nx.bit_length()),)),
             ],
             compiler_params=pltpu.CompilerParams(collective_id=0, has_side_effects=True,
-                                                 vmem_limit_bytes=60 * 1024 * 1024),
-        )(rhs, diag, lift, sflat, basis.T, cflat)
+                                                 vmem_limit_bytes=30000 * 1024),
+        )(*[pltpu.with_memory_space_constraint(x, pltpu.HBM) for x in (rhs, diag, lift, sflat, basis.T, cflat)])
         sol, hess = pl.pallas_call(
             hand_on,
             out_shape=(jax.ShapeDtypeStruct(sol.shape, F32), jax.ShapeDtypeStruct(hess.shape, F32)),
             in_specs=[vm, vm],
             out_specs=(vm, vm),
-            compiler_params=pltpu.CompilerParams(vmem_limit_bytes=60 * 1024 * 1024),
+            compiler_params=pltpu.CompilerParams(vmem_limit_bytes=30000 * 1024),
         )(sol, hess)
         return sol, hess.T
 

time: 27.1 us -> 25.5 us (0.941)
  Pallas kernels: 26.3 us -> 24.7 us
    pallas_call x1, Pallas kernels: 1.57 us -> 0.67 us  [body(): pl.pallas_call(hand_on, out_shape=(jax.ShapeDtypeStruct(sol.shape, F32),...]
    pallas_call x1, Pallas kernels: 24.7 us -> 24 us  [body(): pl.pallas_call(functools.partial(kernel, nx, ny, ti, tj, n, kc), out_shap...]
where the time goes in v1:
time: 25.5 us; the launch traced here: 25.3 us
  Pallas kernels  24.7 us (97%)
  between operations  0.64 us (3%)
    pallas_call x1, Pallas kernels, body(): pl.pallas_call(functools.partial(kernel, nx, ny, ti, tj, n, kc), out_shap...  24 us
    pallas_call x1, Pallas kernels, body(): pl.pallas_call(hand_on, out_shape=(jax.ShapeDtypeStruct(sol.shape, F32),...  0.67 us

profile of v1, /device:TPU:0, one launch (start us, length us, event | category | flops | bytes accessed | tf_op | source)
XLA Modules:
  0.0 25.3 jit_solution(5117628215834341815)
XLA Ops:
  0.6 24.0 %shard_map.77 = (f32[16,16,128]{2,1,0:T(8,128)S(1)}, f32[2,3]{1,0:T(2,128)S(1)}) custom-call(f32[16,16,128]{2,1,0:T(8,128)} %rhs_h.1, bf16[16,16,128,128]{3,2,1,0:T(8,128)(2,1)} %diag.1, bf16[4,128,128]{2,1,0:T(8,128)(2,1)} %lift_h.1, s32[16,4,16]{2,1,0:T(4,128)} %bitcast.7, f32[8,128]{1,0:T(8,128)} %bitcast.8, f32[16,64,16]{2,1,0:T(8,128)} %bitcast.6), custom_call_target="tpu_custom_call" | custom-call | tf_op jit(solution)/shard_map/pallas_call | solution.py:447
  24.7 0.7 %shard_map.78 = (f32[16,16,128]{2,1,0:T(8,128)}, f32[2,3]{1,0:T(2,128)}) custom-call(f32[16,16,128]{2,1,0:T(8,128)S(1)} %get-tuple-element.6.sol_in, f32[2,3]{1,0:T(2,128)S(1)} %get-tuple-element.7.hess_in), custom_call_target="tpu_custom_call" | custom-call | tf_op jit(solution)/shard_map/pallas_call | solution.py:482

commit v2 on v1

--- a/solution.py
+++ b/solution.py
@@ -11,8 +11,26 @@
 BF16 = jnp.bfloat16
 
 
-def hdot(a, b, dims=(((1,), (0,)), ((), ()))):
-    return lax.dot_general(a, b, dims, precision=lax.Precision.HIGHEST, preferred_element_type=F32)
+def fdot(a, b):
+    return jnp.dot(a, b, preferred_element_type=F32)
+
+
+def over_first(a, b):
+    return lax.dot_general(a, b, (((0,), (0,)), ((), ())), preferred_element_type=F32)
+
+
+def cut(x):
+    hi = x.astype(BF16)
+    return hi, (x - hi.astype(F32)).astype(BF16)
+
+
+def fine_dot(x, w):
+    hi, lo = cut(x)
+    return fdot(jnp.concatenate([hi, lo, hi], axis=1), w)
+
+
+def one_hot(x):
+    return x.astype(F32).astype(BF16)
 
 
 def total(x):
@@ -29,7 +47,7 @@
 
 def kernel(nx, ny, ti, tj, n, kc, rhs_h, diag, lift_h, state_h, basis_h, cinv_h, out, hess_out,
            rhs, lift, state, basis, cinv,
-           dvm, wts, masks, cext, wbuf, sends, halos, csend, chalo, sums, msgs,
+           dvm, wts, cwts, wmat, masks, packs, rims, cext, pbuf, zbuf, cbuf, fbuf, gbuf, wbuf, sends, halos, csend, chalo, sums, msgs,
            isem, dsem, ssem, rsem, lsend, lrecv, msend, mrecv, know):
     gx = lax.axis_index("gx")
     gy = lax.axis_index("gy")
@@ -166,13 +184,12 @@
                 c.start()
 
     def broadcast():
-        def one(k, carry):
-            t = lax.rem(me + k, count)
-            pltpu.make_async_remote_copy(
-                src_ref=msgs.at[me], dst_ref=msgs.at[me], send_sem=msend.at[0], recv_sem=mrecv.at[0],
-                device_id=(t // ny, lax.rem(t, ny)), device_id_type=MESH).start()
-            return carry
-        lax.fori_loop(1, count, one, 0)
+        for dx in sorted(range(nx), key=lambda d: abs(d - nx // 2)):
+            for dy in range(ny):
+                if dx or dy:
+                    pltpu.make_async_remote_copy(
+                        src_ref=msgs.at[me], dst_ref=msgs.at[me], send_sem=msend.at[0], recv_sem=mrecv.at[0],
+                        device_id=(lax.rem(gx + dx, nx), lax.rem(gy + dy, ny)), device_id_type=MESH).start()
 
     def bc_wait(which):
         part = msgs.at[pl.ds(0, count - 1)]
@@ -204,75 +221,103 @@
             row = jnp.where(lane1 == p, v, row)
         return row
 
-    e1 = (iota((kc, n), 1) // kc == iota((kc, n), 0)).astype(F32)
-    e3 = (lax.rem(iota((kc, n), 1), kc) == iota((kc, n), 0)).astype(F32)
+    row_k = lax.rem(iota((kc, n), 1), kk) // kc == iota((kc, n), 0)
+    row_l = lax.rem(iota((kc, n), 1), kc) == iota((kc, n), 0)
     pick = iota((ti, n), 1) // kc == iota((ti, n), 0)
+    low = lane1 < kk
     loads[0].wait()
     loads[1].wait()
-    Rt = basis[...]
-    over_first = (((0,), (0,)), ((), ()))
-    RT = hdot(Rt, e3, over_first)
-
-    def packed_rowsum(f3):
-        rows = hdot(jnp.sum(f3, axis=1), RT)
-        return jnp.sum(jnp.where(pick, rows, 0.0), axis=0, keepdims=True)
-
+    Rh, Rl = cut(basis[...])
+
+    def spreads(pattern):
+        e = one_hot(pattern)
+        return over_first(Rh, e).astype(BF16), over_first(Rl, e).astype(BF16)
+
+    def stacked(hi, lo):
+        return jnp.concatenate([hi, hi, lo], axis=0)
+    RT = stacked(*spreads(row_l))
     rhs3 = rhs[...]
     rhs2 = rhs3.reshape(elems, n)
+
+    def packed_rowsum(f3):
+        rows = fine_dot(jnp.sum(f3, axis=1), RT)
+        return jnp.sum(jnp.where(pick, rows, 0.0), axis=0, keepdims=True)
+
     fill_sends(0, rhs)
     sums[0, ny + gy] = packed_rowsum(rhs3)
-
-    pl.semaphore_wait(barrier, near_count)
-    start_all(rim_copies(0))
-    share_lines(0)
     loads[2].wait()
-    cext[...] = jnp.zeros_like(cext)
-    eye = (iota((tj, tj), 0) == iota((tj, tj), 1)).astype(F32)
+    eye = one_hot(iota((tj, tj), 0) == iota((tj, tj), 1))
+    chi, clo = cut(cinv[...])
+    both = jnp.concatenate([chi, clo], axis=2)
+    both = jnp.concatenate([both, both], axis=1).reshape(ti * n, 2 * tj)
+    turned = lax.dot_general(jnp.concatenate([eye, eye], axis=1), both, (((1,), (1,)), ((), ())),
+                             preferred_element_type=F32)
     for q in range(ti):
-        cext[q * tj:(q + 1) * tj, 0:kk] = hdot(eye, cinv[q], (((1,), (1,)), ((), ())))
+        cext[q * tj:(q + 1) * tj] = turned[:, q * n:(q + 1) * n]
     c3d = cext[0:elems].reshape(ti, tj, n)
     csend[0:tj] = c3d[0]
     csend[tj:2 * tj] = c3d[ti - 1]
     csend[2 * tj:2 * tj + ti] = c3d[:, 0, :]
     csend[2 * tj + ti:2 * tj + 2 * ti] = c3d[:, tj - 1, :]
+
+    pl.semaphore_wait(barrier, near_count)
+    start_all(rim_copies(0))
+    share_lines(0)
     start_all(coarse_copies())
 
-    RE = hdot(Rt, e1, over_first)
-    e4 = (lax.rem(iota((n, kc), 0), kc) == iota((n, kc), 1)).astype(F32)
-    RF = hdot(e4, Rt)
-    G = (lax.rem(iota((n, n), 0), kc) == iota((n, n), 1) // kc).astype(F32)
-    flip = (iota((n, n), 0) + iota((n, n), 1) == n - 1).astype(BF16)
+    RE = stacked(*spreads(row_k))
+    row_le = one_hot(row_l)
+    RFh, RFl = over_first(row_le, Rh).astype(BF16), over_first(row_le, Rl).astype(BF16)
+    low_row = iota((n, n), 0) < kk
+    RF = jnp.concatenate([RFh, jnp.where(low_row, RFl.astype(F32), 0.0).astype(BF16)], axis=0)
+    G = one_hot(lax.rem(iota((n, n), 0), kc) == lax.rem(iota((n, n), 1), kk) // kc)
+    G = jnp.concatenate([G, G], axis=0)
+    Q = one_hot(lax.rem(iota((n, n), 0), kc) == lax.rem(iota((n, n), 1), kc))
+    flip = one_hot(iota((n, n), 0) + iota((n, n), 1) == n - 1)
+    RR = jnp.concatenate([RFh, RFl], axis=1)
     loads[4].wait()
     for f in range(4):
-        wts[2 * f * n:(2 * f + 1) * n] = lift[f]
-        wts[(2 * f + 1) * n:(2 * f + 2) * n] = jnp.dot(flip, lift[f], preferred_element_type=F32).astype(BF16)
+        straight = lift[f]
+        turned = fdot(flip, straight).astype(BF16)
+        wts[2 * f * n:(2 * f + 1) * n] = straight
+        wts[(2 * f + 1) * n:(2 * f + 2) * n] = turned
+        pair = jnp.concatenate([straight, turned], axis=1)
+        prod = fdot(RR, jnp.concatenate([pair, pair], axis=0))
+        cwts[f * n:(f + 1) * n] = jnp.where(low_row, prod[:, 0:n], prod[:, n:2 * n]).astype(BF16)
     loads[3].wait()
     own_j = lax.rem(iota((elems, tj), 0), tj) == iota((elems, tj), 1)
     ones = jnp.ones((tj, n), BF16)
     for f in range(4):
         rows = state[:, f, :].astype(F32)
         wide = jnp.broadcast_to(rows[:, None, :], (ti, tj, tj)).reshape(elems, tj)
-        col = jnp.dot(jnp.where(own_j, wide, 0.0).astype(BF16), ones, preferred_element_type=F32)
-        masks[2 * f] = (col == 1.0).astype(F32)
-        masks[2 * f + 1] = (col == 2.0).astype(F32)
+        col = fdot(jnp.where(own_j, wide, 0.0).astype(BF16), ones)
+        masks[2 * f] = one_hot(col == 1.0)
+        masks[2 * f + 1] = one_hot(col == 2.0)
+        packs[f] = (col == jnp.where(low, 1.0, 2.0)).astype(F32)
+        if f >= 2:
+            edge = col.reshape(ti, tj, n)[:, 0 if f == 2 else tj - 1, :]
+            rims[2 * f - 4] = one_hot(edge == 1.0)
+            rims[2 * f - 3] = one_hot(edge == 2.0)
 
     hrow = iota((hrows, 1), 0)
     valid = jnp.where(hrow < o_s, n_i, jnp.where(hrow < o_w, s_i, jnp.where(
         hrow < o_e, w_i, jnp.where(hrow < o_nw, e_i, jnp.where(
             hrow < o_ne, n_i * w_i, jnp.where(hrow < o_sw, n_i * e_i, jnp.where(
                 hrow < o_se, s_i * w_i, s_i * e_i))))))) > 0
+    ok_rim = jnp.concatenate([valid[o_n:o_w], valid[o_w:o_w + ti], valid[o_e:o_e + ti]], axis=0)
 
     jrow = lax.rem(iota((elems, 1), 0), tj)
     trow = iota((tj, 1), 0)
+    inner = 1.0 + 0.25 * ((jrow > 0).astype(F32) + (jrow < tj - 1).astype(F32))
 
     def spread(col):
         return jnp.broadcast_to(col[:, None, :], (ti, tj, n)).reshape(elems, n)
 
     def left_of(x, edge):
-        return jnp.where(jrow == 0, spread(edge), pltpu.roll(x, 1, 0))
+        return jnp.where(jrow == 0, edge, pltpu.roll(x, 1, 0))
 
     def right_of(x, edge):
-        return jnp.where(jrow == tj - 1, spread(edge), pltpu.roll(x, elems - 1, 0))
+        return jnp.where(jrow == tj - 1, edge, pltpu.roll(x, elems - 1, 0))
 
     def line_sum(g, d):
         acc = sums[g, (d + 1) * ny]
@@ -280,28 +325,74 @@
             acc = acc + sums[g, (d + 1) * ny + q]
         return acc
 
-    def three_lines(g):
-        return line_sum(g, 0), line_sum(g, -1), line_sum(g, 1)
-
-    def precondition(f_own, f_halo, lines, coarse):
-        p_c, p_n, p_s = lines
+    half = tj // 2
+    keep = [one_hot(lax.rem(iota((2 * tj, n), 0), half) == t) for t in range(half)]
+    none = jnp.zeros((kc, n), BF16)
+    coarse_rows = jnp.concatenate([
+        jnp.concatenate([Rh, none], axis=1), jnp.concatenate([none, Rh], axis=1)], axis=0)
+    own_block = (iota((tj, n), 1) // kc == iota((tj, n), 0)).astype(F32)
+
+    def local_lifts(x):
+        b = x.astype(BF16)
+        gap = jnp.zeros((tj, n), BF16)
+        nb = [
+            jnp.concatenate([gap, b[0:elems - tj]], axis=0),
+            jnp.concatenate([b[tj:], gap], axis=0),
+            left_of(x, 0.0).astype(BF16),
+            right_of(x, 0.0).astype(BF16),
+        ]
+        cols = []
+        for f in range(4):
+            cols.append(nb[f] * masks[2 * f])
+            cols.append(nb[f] * masks[2 * f + 1])
+        wbuf[...] = fdot(jnp.concatenate(cols, axis=1), wts[...]).reshape(ti, tj, n)
+
+    def local_blocks(x, first):
+        for q in range(ti):
+            if first:
+                dcopies[q].wait()
+            both = jnp.concatenate(cut(x[q * tj:(q + 1) * tj]), axis=0)
+            rhs_w = jnp.concatenate(
+                [dvm[q, 0:half].reshape(half * n, n), dvm[q, half:tj].reshape(half * n, n)], axis=1)
+            if first:
+                prod = None
+                for t in range(0, half, 2):
+                    lhs = jnp.concatenate([
+                        jnp.concatenate([both * keep[t], both * keep[t + 1]], axis=1), coarse_rows], axis=0)
+                    part = fdot(lhs, rhs_w[t * n:(t + 2) * n])
+                    prod = part[0:2 * tj] if prod is None else prod + part[0:2 * tj]
+                    for side in range(2):
+                        at = (side * half + t) * kc
+                        hi, lo = cut(part[2 * tj:, side * n:(side + 1) * n])
+                        wmat[q, at:at + 2 * kc, 0:n] = hi
+                        wmat[q, at:at + 2 * kc, n:2 * n] = lo
+            else:
+                prod = fdot(jnp.concatenate([both * keep[t] for t in range(half)], axis=1), rhs_w)
+            prod = prod[0:tj] + prod[tj:2 * tj]
+            wbuf[q] += jnp.concatenate([prod[0:half, 0:n], prod[half:tj, n:2 * n]], axis=0)
+
+    def local_coarse(x):
+        c = fine_dot(x, RE)
+        cbuf[...] = c + 0.25 * (left_of(c, 0.0) + right_of(c, 0.0))
+        c3 = c.reshape(ti, tj, n)
+        return c3[:, 0, :], c3[:, tj - 1, :]
+
+    def fix(g, own_w, own_e):
+        p_c, p_n, p_s = line_sum(g, 0), line_sum(g, -1), line_sum(g, 1)
+        f_halo = jnp.where(valid, halos[g], 0.0)
         stack = jnp.concatenate([
             jnp.where(pick, jnp.broadcast_to(p_c, (ti, n)), 0.0),
             jnp.broadcast_to(jnp.where(lane1 // kc == ti - 1, p_n, 0.0), (8, n)),
             jnp.broadcast_to(jnp.where(lane1 // kc == 0, p_s, 0.0), (8, n))], axis=0)
-        mean = hdot(stack, G) * (1.0 / (ny * tj))
+        mean = fdot(jnp.concatenate(cut(stack), axis=1), G) * (1.0 / (ny * tj))
         m_c, m_n, m_s = mean[0:ti], mean[ti:ti + 1], mean[ti + 8:ti + 9]
-        c_own = coarse - spread(m_c)
-        c_halo = hdot(f_halo, RE)
         m_halo = jnp.concatenate([
             jnp.broadcast_to(m_n, (tj, n)), jnp.broadcast_to(m_s, (tj, n)), m_c, m_c, m_c, m_c,
             jnp.broadcast_to(m_n, (16, n)), jnp.broadcast_to(m_s, (16, n))], axis=0)
-        c_halo = jnp.where(valid, c_halo - m_halo, 0.0)
+        c_halo = jnp.where(valid, fine_dot(f_halo, RE) - m_halo, 0.0)
         c_w1, c_w2 = c_halo[o_w:o_w + ti], c_halo[o_w + ti:o_e]
         c_e1, c_e2 = c_halo[o_e:o_e + ti], c_halo[o_e + ti:o_nw]
         c_n, c_s = c_halo[o_n:o_n + tj], c_halo[o_s:o_s + tj]
-        c3 = c_own.reshape(ti, tj, n)
-        s_own = c_own + 0.25 * (left_of(c_own, c_w1) + right_of(c_own, c_e1))
 
         def row_smooth(x, lo, hi):
             left = jnp.where(trow == 0, lo, pltpu.roll(x, 1, 0))
@@ -309,42 +400,56 @@
             return x + 0.25 * (left + right)
         s_n = row_smooth(c_n, c_halo[o_nw:o_nw + 1], c_halo[o_ne:o_ne + 1])
         s_s = row_smooth(c_s, c_halo[o_sw:o_sw + 1], c_halo[o_se:o_se + 1])
-        s_w = c_w1 + 0.25 * (c_w2 + c3[:, 0, :])
-        s_e = c_e1 + 0.25 * (c3[:, tj - 1, :] + c_e2)
-        z_own = f_own + hdot(s_own * cext[0:elems], RF)
-        f_rim = jnp.concatenate([f_halo[o_n:o_w], f_halo[o_w:o_w + ti], f_halo[o_e:o_e + ti]], axis=0)
-        ok_rim = jnp.concatenate([valid[o_n:o_w], valid[o_w:o_w + ti], valid[o_e:o_e + ti]], axis=0)
+        s_w = c_w1 + 0.25 * (c_w2 + own_w - m_c)
+        s_e = c_e1 + 0.25 * (own_e - m_c + c_e2)
+        s_own = cbuf[...] - inner * spread(m_c)
+        s_own = s_own + jnp.where(jrow == 0, spread(0.25 * c_w1), 0.0) + jnp.where(
+            jrow == tj - 1, spread(0.25 * c_e1), 0.0)
+        p = s_own * cext[0:elems]
+        pbuf[g] = p
         s_rim = jnp.concatenate([s_n, s_s, s_w, s_e], axis=0)
-        z_rim = jnp.where(ok_rim, f_rim + hdot(s_rim * cext[elems:elems + h], RF), 0.0)
-        return z_own, z_rim
-
-    def operator(z, z_rim):
+        p_rim = jnp.where(ok_rim, s_rim * cext[elems:elems + h], 0.0)
+
+        hi, lo = cut(p)
+        coef = fdot(jnp.where(low, hi.astype(F32), lo.astype(F32)).astype(BF16), Q)
         nb = [
-            jnp.concatenate([z_rim[0:tj], z[0:elems - tj]], axis=0),
-            jnp.concatenate([z[tj:], z_rim[tj:2 * tj]], axis=0),
-            left_of(z, z_rim[2 * tj:2 * tj + ti]),
-            right_of(z, z_rim[2 * tj + ti:2 * tj + 2 * ti]),
+            jnp.concatenate([p_rim[0:tj], p[0:elems - tj]], axis=0),
+            jnp.concatenate([p[tj:], p_rim[tj:2 * tj]], axis=0),
+            left_of(p, spread(p_rim[2 * tj:2 * tj + ti])),
+            right_of(p, spread(p_rim[2 * tj + ti:2 * tj + 2 * ti])),
         ]
-        cols = []
-        for f in range(4):
-            cols.append((nb[f] * masks[2 * f]).astype(BF16))
-            cols.append((nb[f] * masks[2 * f + 1]).astype(BF16))
-        lifted = jnp.dot(jnp.concatenate(cols, axis=1), wts[...], preferred_element_type=F32)
-        wbuf[...] = lifted.reshape(ti, tj, n)
-        half = tj // 2
+        cols = [(nb[f] * packs[f]).astype(BF16) for f in range(4)]
+        lifted = fdot(jnp.concatenate(cols, axis=1), cwts[...])
+
+        def rim_lift(f, at, one, two):
+            b = f_halo[at:at + 16].astype(BF16)
+            return fdot(jnp.concatenate([b * one, b * two], axis=1), wts[2 * f * n:(2 * f + 2) * n])
+        last = elems - tj
+        north = rim_lift(0, o_n, masks[0, 0:tj], masks[1, 0:tj])
+        south = rim_lift(1, o_s, masks[2, last:elems], masks[3, last:elems])
+        west = rim_lift(2, o_w, rims[0], rims[1])
+        east = rim_lift(3, o_e, rims[2], rims[3])
         for q in range(ti):
-            a = z[q * tj:(q + 1) * tj]
-            hi = a.astype(BF16)
-            both = jnp.concatenate([hi, (a - hi.astype(F32)).astype(BF16)], axis=0)
-            lhs = jnp.concatenate([both * keep[t] for t in range(half)], axis=1)
-            rhs_w = jnp.concatenate(
-                [dvm[q, 0:half].reshape(half * n, n), dvm[q, half:tj].reshape(half * n, n)], axis=1)
-            prod = jnp.dot(lhs, rhs_w, preferred_element_type=F32)
-            prod = prod[0:tj] + prod[tj:2 * tj]
-            wbuf[q] += jnp.concatenate([prod[0:half, 0:n], prod[half:tj, n:2 * n]], axis=0)
-
-    keep = [(lax.rem(iota((2 * tj, n), 0), tj // 2) == t).astype(F32).astype(BF16) for t in range(tj // 2)]
-    coarse_rhs = hdot(rhs2, RE)
+            at = slice(q * tj, (q + 1) * tj)
+            x = jnp.concatenate(cut(coef[at] * own_block), axis=1)
+            w = wmat[q]
+            y = fdot(x, jnp.concatenate([w, w], axis=0))
+            y = y[:, 0:n] + y[:, n:2 * n] + lifted[at]
+            if q == 0:
+                y = y + north
+            if q == ti - 1:
+                y = y + south
+            side = jnp.where(trow == 0, west[q:q + 1], jnp.where(trow == tj - 1, east[q:q + 1], 0.0))
+            wbuf[q] += y + side
+
+    def full(g, x):
+        hi, lo = cut(pbuf[g])
+        mixed = jnp.where(low, hi.astype(F32), lo.astype(F32)).astype(BF16)
+        zbuf[g] = x + fdot(jnp.concatenate([mixed, hi], axis=1), RF)
+
+    edges = local_coarse(rhs2)
+    local_lifts(rhs2)
+    local_blocks(rhs2, True)
     line_wait(0, "recv")
     rim_wait(0, "recv")
     rim_wait(2, "recv")
@@ -352,35 +457,38 @@
         tell(0)
 
     cext[elems:elems + h] = chalo[...]
-    z1, z1_rim = precondition(rhs2, jnp.where(valid, halos[0], 0.0), three_lines(0), coarse_rhs)
-    for c in dcopies:
-        c.wait()
-    operator(z1, z1_rim)
+    fix(0, *edges)
     fill_sends(1, wbuf)
     start_all(rim_copies(1))
     sums[1, ny + gy] = packed_rowsum(wbuf[...])
     share_lines(1)
     w1 = wbuf[...].reshape(elems, n)
+    fbuf[...] = w1
     for q in range(len(steps)):
         learn(q)
         if q + 1 < len(steps):
             tell(q + 1)
+    edges = local_coarse(w1)
+    local_lifts(w1)
+    local_blocks(w1, False)
     own_n1 = total(rhs2 * rhs2)
     p_one = safe_div(total(rhs2 * w1), own_n1)
     gap = w1 - p_one * rhs2
+    gbuf[...] = gap
     own_n2 = total(gap * gap)
-    coarse_w = hdot(w1, RE)
     line_wait(1, "recv")
     rim_wait(1, "recv")
 
-    z2, z2_rim = precondition(w1, jnp.where(valid, halos[1], 0.0), three_lines(1), coarse_w)
-    operator(z2, z2_rim)
+    fix(1, *edges)
     w2 = wbuf[...].reshape(elems, n)
+    rhs2, gap = rhs[...].reshape(elems, n), gbuf[...]
     p_two = safe_div(total(rhs2 * w2), own_n1)
     q_two = safe_div(total(gap * w2), own_n2)
     rest = w2 - p_two * rhs2 - q_two * gap
     msgs[me] = message([own_n1, p_one, own_n2, p_two, q_two, total(rest * rest)])
     broadcast()
+    full(0, rhs2)
+    full(1, fbuf[...])
     bc_wait("recv")
     Y = msgs[:, 0, :]
     l_n1, l_p, l_n2, l_a, l_b, l_n3 = [Y[:, q:q + 1] for q in range(6)]
@@ -414,7 +522,7 @@
     y1 = (cos_one * start_len - upper * y2) / first
     c2 = y2 / gap_len
     c1 = y1 / start_len - c2 * h11
-    out[...] = (c1 * z1 + c2 * z2).reshape(ti, tj, n)
+    out[...] = (c1 * zbuf[0] + c2 * zbuf[1]).reshape(ti, tj, n)
     hr, hc = iota((2, 3), 1), iota((2, 3), 0)
     hess_out[...] = jnp.where(
         hr == 0, jnp.where(hc == 0, h11, h12),
@@ -457,8 +565,17 @@
                 pltpu.VMEM((ti, kc * kc, tj), F32),
                 pltpu.VMEM((ti, tj, n, n), BF16),
                 pltpu.VMEM((8 * n, n), BF16),
-                pltpu.VMEM((8, ti * tj, n), F32),
+                pltpu.VMEM((4 * n, n), BF16),
+                pltpu.VMEM((ti, tj * kc, 2 * n), BF16),
+                pltpu.VMEM((8, ti * tj, n), BF16),
+                pltpu.VMEM((4, ti * tj, n), F32),
+                pltpu.VMEM((4, ti, n), BF16),
                 pltpu.VMEM((ti * tj + h, n), F32),
+                pltpu.VMEM((2, ti * tj, n), F32),
+                pltpu.VMEM((2, ti * tj, n), F32),
+                pltpu.VMEM((ti * tj, n), F32),
+                pltpu.VMEM((ti * tj, n), F32),
+                pltpu.VMEM((ti * tj, n), F32),
                 pltpu.VMEM((ti, tj, n), F32),
                 pltpu.VMEM((2, hrows, n), F32),
                 pltpu.VMEM((2, hrows, n), F32),

time: 25.5 us -> 23.9 us (0.937)
  Pallas kernels: 24.7 us -> 23.1 us
    pallas_call x1, Pallas kernels: 24 us -> 22.4 us  [body(): pl.pallas_call(functools.partial(kernel, nx, ny, ti, tj, n, kc), out_shap...]
where the time goes in v2:
time: 23.9 us; the launch traced here: 23.7 us
  Pallas kernels  23.1 us (97%)
  between operations  0.64 us (3%)
    pallas_call x1, Pallas kernels, body(): pl.pallas_call(functools.partial(kernel, nx, ny, ti, tj, n, kc), out_shap...  22.4 us
    pallas_call x1, Pallas kernels, body(): pl.pallas_call(hand_on, out_shape=(jax.ShapeDtypeStruct(sol.shape, F32),...  0.67 us

profile of v2, /device:TPU:0, one launch (start us, length us, event | category | flops | bytes accessed | tf_op | source)
XLA Modules:
  0.0 23.7 jit_solution(5098577822704211131)
XLA Ops:
  0.6 22.4 %shard_map.77 = (f32[16,16,128]{2,1,0:T(8,128)S(1)}, f32[2,3]{1,0:T(2,128)S(1)}) custom-call(f32[16,16,128]{2,1,0:T(8,128)} %rhs_h.1, bf16[16,16,128,128]{3,2,1,0:T(8,128)(2,1)} %diag.1, bf16[4,128,128]{2,1,0:T(8,128)(2,1)} %lift_h.1, s32[16,4,16]{2,1,0:T(4,128)} %bitcast.7, f32[8,128]{1,0:T(8,128)} %bitcast.8, f32[16,64,16]{2,1,0:T(8,128)} %bitcast.6), custom_call_target="tpu_custom_call" | custom-call | tf_op jit(solution)/shard_map/pallas_call | solution.py:555
  23.0 0.7 %shard_map.78 = (f32[16,16,128]{2,1,0:T(8,128)}, f32[2,3]{1,0:T(2,128)}) custom-call(f32[16,16,128]{2,1,0:T(8,128)S(1)} %get-tuple-element.6.sol_in, f32[2,3]{1,0:T(2,128)S(1)} %get-tuple-element.7.hess_in), custom_call_target="tpu_custom_call" | custom-call | tf_op jit(solution)/shard_map/pallas_call | solution.py:599

commit v3 on v2

--- a/solution.py
+++ b/solution.py
@@ -27,6 +27,18 @@
 def fine_dot(x, w):
     hi, lo = cut(x)
     return fdot(jnp.concatenate([hi, lo, hi], axis=1), w)
+
+
+def exact_dot(x, w):
+    m = x.shape[0]
+    y = fdot(jnp.concatenate(cut(x), axis=0), w)
+    return y[0:m] + y[m:2 * m]
+
+
+def small_dot(x, w):
+    m, n = x.shape[0], w.shape[1] // 2
+    y = fdot(jnp.concatenate(cut(x), axis=0), w)
+    return y[0:m, 0:n] + y[m:2 * m, 0:n] + y[0:m, n:2 * n]
 
 
 def one_hot(x):
@@ -56,20 +68,12 @@
     elems = ti * tj
     kk = kc * kc
 
-    loads = [pltpu.make_async_copy(a, b, isem.at[q]) for q, (a, b) in enumerate(
-        ((rhs_h, rhs), (basis_h, basis), (cinv_h, cinv), (state_h, state), (lift_h, lift)))]
-    for c in loads:
-        c.start()
-    dcopies = [pltpu.make_async_copy(diag.at[q], dvm.at[q], dsem.at[q]) for q in range(ti)]
-    for c in dcopies:
-        c.start()
-
     barrier = pltpu.get_barrier_semaphore()
 
     has_n, has_s, has_w, has_e = gx > 0, gx < nx - 1, gy > 0, gy < ny - 1
     n_i, s_i, w_i, e_i = [v.astype(jnp.int32) for v in (has_n, has_s, has_w, has_e)]
-    near = [(has_n, -1, k) for k in range(ny)] + [(has_s, 1, k) for k in range(ny)] + [
-        (None, 0, k) for k in range(1, ny)]
+    near = [(has_s, 1, k) for k in range(ny)] + [(None, 0, k) for k in range(1, ny)] + [
+        (has_n, -1, k) for k in range(ny)]
     near_count = ny - 1 + ny * (n_i + s_i)
 
     def when(ok, run):
@@ -79,10 +83,21 @@
             pl.when(ok)(run)
 
     sums[...] = jnp.zeros_like(sums)
+    halos[...] = jnp.zeros_like(halos)
+    chalo[...] = jnp.zeros_like(chalo)
     for ok, d, k in near:
         def hello(d=d, k=k):
             pl.semaphore_signal(barrier, inc=1, device_id=(gx + d, lax.rem(gy + k, ny)), device_id_type=MESH)
         when(ok, hello)
+
+    loads = [pltpu.make_async_copy(a, b, isem.at[q]) for q, (a, b) in enumerate(
+        ((rhs_h, rhs), (basis_h, basis), (cinv_h, cinv), (state_h, state), (lift_h, lift)))]
+    for c in loads:
+        c.start()
+    group = max(1, ti // 4)
+    dcopies = [pltpu.make_async_copy(diag.at[pl.ds(q, group)], dvm.at[pl.ds(q, group)], dsem.at[q // group])
+               for q in range(0, ti, group)]
+    dcopies[0].start()
 
     steps = []
     r = 2
@@ -126,33 +141,19 @@
             when(ok, one)
 
     h = 2 * ti + 2 * tj
-    o_n, o_s, o_w, o_e = 0, tj, 2 * tj, 2 * tj + 2 * ti
-    o_nw = 2 * tj + 4 * ti
-    o_ne, o_sw, o_se = o_nw + 8, o_nw + 16, o_nw + 24
-    hrows = o_nw + 32
-    routes = [
-        (has_n, (gx - 1, gy), o_n, o_s, tj),
-        (has_s, (gx + 1, gy), o_s, o_n, tj),
-        (has_w, (gx, gy - 1), o_w, o_e, 2 * ti),
-        (has_e, (gx, gy + 1), o_e, o_w, 2 * ti),
-        (jnp.logical_and(has_n, has_w), (gx - 1, gy - 1), o_nw, o_se, 8),
-        (jnp.logical_and(has_n, has_e), (gx - 1, gy + 1), o_ne, o_sw, 8),
-        (jnp.logical_and(has_s, has_w), (gx + 1, gy - 1), o_sw, o_ne, 8),
-        (jnp.logical_and(has_s, has_e), (gx + 1, gy + 1), o_se, o_nw, 8),
-    ]
     croutes = [
         (has_n, (gx - 1, gy), 0, tj, tj),
         (has_s, (gx + 1, gy), tj, 0, tj),
         (has_w, (gx, gy - 1), 2 * tj, 2 * tj + ti, ti),
         (has_e, (gx, gy + 1), 2 * tj + ti, 2 * tj, ti),
     ]
-    opposite = [1, 0, 3, 2, 7, 6, 5, 4]
+    opposite = [1, 0, 3, 2]
 
     def rim_copies(g):
         return [(ok, pltpu.make_async_remote_copy(
             src_ref=sends.at[g, pl.ds(src, rows)], dst_ref=halos.at[g, pl.ds(dst, rows)],
             send_sem=ssem.at[g, d], recv_sem=rsem.at[g, opposite[d]],
-            device_id=dev, device_id_type=MESH)) for d, (ok, dev, src, dst, rows) in enumerate(routes)]
+            device_id=dev, device_id_type=MESH)) for d, (ok, dev, src, dst, rows) in enumerate(croutes)]
 
     def coarse_copies():
         return [(ok, pltpu.make_async_remote_copy(
@@ -161,8 +162,7 @@
             device_id=dev, device_id_type=MESH)) for d, (ok, dev, src, dst, rows) in enumerate(croutes)]
 
     def rim_wait(g, which):
-        table = routes if g < 2 else croutes
-        for d, (ok, dev, src, dst, rows) in enumerate(table):
+        for d, (ok, dev, src, dst, rows) in enumerate(croutes):
             @pl.when(ok)
             def _(d=d, dev=dev, src=src, rows=rows):
                 if g < 2:
@@ -184,12 +184,12 @@
                 c.start()
 
     def broadcast():
-        for dx in sorted(range(nx), key=lambda d: abs(d - nx // 2)):
-            for dy in range(ny):
-                if dx or dy:
-                    pltpu.make_async_remote_copy(
-                        src_ref=msgs.at[me], dst_ref=msgs.at[me], send_sem=msend.at[0], recv_sem=mrecv.at[0],
-                        device_id=(lax.rem(gx + dx, nx), lax.rem(gy + dy, ny)), device_id_type=MESH).start()
+        for tx, ty in sorted(((x, y) for x in range(nx) for y in range(ny)), key=lambda t: t[0] // 2 + t[1] // 2 + t[1] % 2):
+            @pl.when(jnp.logical_or(gx != tx, gy != ty))
+            def _(tx=tx, ty=ty):
+                pltpu.make_async_remote_copy(
+                    src_ref=msgs.at[me], dst_ref=msgs.at[me], send_sem=msend.at[0], recv_sem=mrecv.at[0],
+                    device_id=(tx, ty), device_id_type=MESH).start()
 
     def bc_wait(which):
         part = msgs.at[pl.ds(0, count - 1)]
@@ -202,16 +202,10 @@
             c.wait_recv()
 
     def fill_sends(g, ref):
-        sends[g, o_n:o_n + tj] = ref[0]
-        sends[g, o_s:o_s + tj] = ref[ti - 1]
-        sends[g, o_w:o_w + ti] = ref[:, 0, :]
-        sends[g, o_w + ti:o_w + 2 * ti] = ref[:, 1, :]
-        sends[g, o_e:o_e + ti] = ref[:, tj - 1, :]
-        sends[g, o_e + ti:o_e + 2 * ti] = ref[:, tj - 2, :]
-        sends[g, o_nw:o_nw + 8] = jnp.broadcast_to(ref[0, 0:1, :], (8, n))
-        sends[g, o_ne:o_ne + 8] = jnp.broadcast_to(ref[0, tj - 1:tj, :], (8, n))
-        sends[g, o_sw:o_sw + 8] = jnp.broadcast_to(ref[ti - 1, 0:1, :], (8, n))
-        sends[g, o_se:o_se + 8] = jnp.broadcast_to(ref[ti - 1, tj - 1:tj, :], (8, n))
+        sends[g, 0:tj] = ref[0].astype(BF16)
+        sends[g, tj:2 * tj] = ref[ti - 1].astype(BF16)
+        sends[g, 2 * tj:2 * tj + ti] = ref[:, 0, :].astype(BF16)
+        sends[g, 2 * tj + ti:h] = ref[:, tj - 1, :].astype(BF16)
 
     lane1 = iota((1, n), 1)
 
@@ -224,6 +218,7 @@
     row_k = lax.rem(iota((kc, n), 1), kk) // kc == iota((kc, n), 0)
     row_l = lax.rem(iota((kc, n), 1), kc) == iota((kc, n), 0)
     pick = iota((ti, n), 1) // kc == iota((ti, n), 0)
+    pick_j = iota((tj, n), 1) // kc == iota((tj, n), 0)
     low = lane1 < kk
     loads[0].wait()
     loads[1].wait()
@@ -235,16 +230,21 @@
 
     def stacked(hi, lo):
         return jnp.concatenate([hi, hi, lo], axis=0)
-    RT = stacked(*spreads(row_l))
+    RT = jnp.concatenate(spreads(row_l), axis=1)
     rhs3 = rhs[...]
     rhs2 = rhs3.reshape(elems, n)
 
-    def packed_rowsum(f3):
-        rows = fine_dot(jnp.sum(f3, axis=1), RT)
-        return jnp.sum(jnp.where(pick, rows, 0.0), axis=0, keepdims=True)
+    def fill_sums(g, ref):
+        rows = jnp.concatenate([
+            jnp.sum(ref[...], axis=1), ref[:, 0, :], ref[:, 1, :], ref[:, tj - 1, :], ref[:, tj - 2, :],
+            ref[0], ref[ti - 1]], axis=0)
+        rows = small_dot(rows, RT)
+        for q in range(7):
+            at, lanes, size = (q * ti, pick, ti) if q < 5 else (5 * ti + (q - 5) * tj, pick_j, tj)
+            sums[g, ny + gy, q:q + 1] = jnp.sum(jnp.where(lanes, rows[at:at + size], 0.0), axis=0, keepdims=True)
 
     fill_sends(0, rhs)
-    sums[0, ny + gy] = packed_rowsum(rhs3)
+    fill_sums(0, rhs)
     loads[2].wait()
     eye = one_hot(iota((tj, tj), 0) == iota((tj, tj), 1))
     chi, clo = cut(cinv[...])
@@ -265,13 +265,14 @@
     share_lines(0)
     start_all(coarse_copies())
 
+    for c in dcopies[1:]:
+        c.start()
     RE = stacked(*spreads(row_k))
     row_le = one_hot(row_l)
     RFh, RFl = over_first(row_le, Rh).astype(BF16), over_first(row_le, Rl).astype(BF16)
     low_row = iota((n, n), 0) < kk
     RF = jnp.concatenate([RFh, jnp.where(low_row, RFl.astype(F32), 0.0).astype(BF16)], axis=0)
     G = one_hot(lax.rem(iota((n, n), 0), kc) == lax.rem(iota((n, n), 1), kk) // kc)
-    G = jnp.concatenate([G, G], axis=0)
     Q = one_hot(lax.rem(iota((n, n), 0), kc) == lax.rem(iota((n, n), 1), kc))
     flip = one_hot(iota((n, n), 0) + iota((n, n), 1) == n - 1)
     RR = jnp.concatenate([RFh, RFl], axis=1)
@@ -299,15 +300,9 @@
             rims[2 * f - 4] = one_hot(edge == 1.0)
             rims[2 * f - 3] = one_hot(edge == 2.0)
 
-    hrow = iota((hrows, 1), 0)
-    valid = jnp.where(hrow < o_s, n_i, jnp.where(hrow < o_w, s_i, jnp.where(
-        hrow < o_e, w_i, jnp.where(hrow < o_nw, e_i, jnp.where(
-            hrow < o_ne, n_i * w_i, jnp.where(hrow < o_sw, n_i * e_i, jnp.where(
-                hrow < o_se, s_i * w_i, s_i * e_i))))))) > 0
-    ok_rim = jnp.concatenate([valid[o_n:o_w], valid[o_w:o_w + ti], valid[o_e:o_e + ti]], axis=0)
-
     jrow = lax.rem(iota((elems, 1), 0), tj)
     trow = iota((tj, 1), 0)
+    scale = 1.0 / (ny * tj)
     inner = 1.0 + 0.25 * ((jrow > 0).astype(F32) + (jrow < tj - 1).astype(F32))
 
     def spread(col):
@@ -320,10 +315,14 @@
         return jnp.where(jrow == tj - 1, edge, pltpu.roll(x, elems - 1, 0))
 
     def line_sum(g, d):
-        acc = sums[g, (d + 1) * ny]
+        acc = sums[g, (d + 1) * ny, 0:1]
         for q in range(1, ny):
-            acc = acc + sums[g, (d + 1) * ny + q]
+            acc = acc + sums[g, (d + 1) * ny + q, 0:1]
         return acc
+
+    def part_of(g, dx, dy, row):
+        at = (dx + 1) * ny + jnp.clip(gy + dy, 0, ny - 1)
+        return sums[g, at, row:row + 1]
 
     half = tj // 2
     keep = [one_hot(lax.rem(iota((2 * tj, n), 0), half) == t) for t in range(half)]
@@ -349,8 +348,8 @@
 
     def local_blocks(x, first):
         for q in range(ti):
-            if first:
-                dcopies[q].wait()
+            if first and q % group == 0:
+                dcopies[q // group].wait()
             both = jnp.concatenate(cut(x[q * tj:(q + 1) * tj]), axis=0)
             rhs_w = jnp.concatenate(
                 [dvm[q, 0:half].reshape(half * n, n), dvm[q, half:tj].reshape(half * n, n)], axis=1)
@@ -378,28 +377,41 @@
         return c3[:, 0, :], c3[:, tj - 1, :]
 
     def fix(g, own_w, own_e):
-        p_c, p_n, p_s = line_sum(g, 0), line_sum(g, -1), line_sum(g, 1)
-        f_halo = jnp.where(valid, halos[g], 0.0)
+        group_of = lane1 // kc
+
+        def lanes(x, mask):
+            return jnp.where(mask, jnp.broadcast_to(x, mask.shape), 0.0)
+        single = [
+            (line_sum(g, -1), ti - 1), (line_sum(g, 1), 0),
+            (part_of(g, -1, -1, 6), tj - 1), (part_of(g, -1, 1, 6), 0),
+            (part_of(g, 1, -1, 5), tj - 1), (part_of(g, 1, 1, 5), 0)]
+        srow = iota((8, n), 0)
+        singles = jnp.zeros((8, n), F32)
+        for q, (x, at) in enumerate(single):
+            singles = jnp.where(jnp.logical_and(srow == q, group_of == at), jnp.broadcast_to(x, (8, n)), singles)
         stack = jnp.concatenate([
-            jnp.where(pick, jnp.broadcast_to(p_c, (ti, n)), 0.0),
-            jnp.broadcast_to(jnp.where(lane1 // kc == ti - 1, p_n, 0.0), (8, n)),
-            jnp.broadcast_to(jnp.where(lane1 // kc == 0, p_s, 0.0), (8, n))], axis=0)
-        mean = fdot(jnp.concatenate(cut(stack), axis=1), G) * (1.0 / (ny * tj))
-        m_c, m_n, m_s = mean[0:ti], mean[ti:ti + 1], mean[ti + 8:ti + 9]
-        m_halo = jnp.concatenate([
-            jnp.broadcast_to(m_n, (tj, n)), jnp.broadcast_to(m_s, (tj, n)), m_c, m_c, m_c, m_c,
-            jnp.broadcast_to(m_n, (16, n)), jnp.broadcast_to(m_s, (16, n))], axis=0)
-        c_halo = jnp.where(valid, fine_dot(f_halo, RE) - m_halo, 0.0)
-        c_w1, c_w2 = c_halo[o_w:o_w + ti], c_halo[o_w + ti:o_e]
-        c_e1, c_e2 = c_halo[o_e:o_e + ti], c_halo[o_e + ti:o_nw]
-        c_n, c_s = c_halo[o_n:o_n + tj], c_halo[o_s:o_s + tj]
+            lanes(line_sum(g, 0) * scale, pick),
+            lanes(part_of(g, 0, -1, 3), pick), lanes(part_of(g, 0, -1, 4), pick),
+            lanes(part_of(g, 0, 1, 1), pick), lanes(part_of(g, 0, 1, 2), pick),
+            lanes(part_of(g, -1, 0, 6), pick_j), lanes(part_of(g, 1, 0, 5), pick_j), singles], axis=0)
+        wide = exact_dot(stack, G)
+        m_c, c_w1, c_w2, c_e1, c_e2 = [wide[q * ti:(q + 1) * ti] for q in range(5)]
+        c_n, c_s = wide[5 * ti:5 * ti + tj], wide[5 * ti + tj:5 * ti + 2 * tj]
+        one = wide[5 * ti + 2 * tj:]
+        m_n, m_s = one[0:1] * scale, one[1:2] * scale
+        c_nw, c_ne, c_sw, c_se = [one[q:q + 1] for q in range(2, 6)]
+        w_f, e_f = w_i.astype(F32), e_i.astype(F32)
+        c_w1, c_w2 = (c_w1 - m_c) * w_f, c_w2 - m_c
+        c_e1, c_e2 = (c_e1 - m_c) * e_f, c_e2 - m_c
+        c_n, c_s = c_n - m_n, c_s - m_s
+        c_nw, c_sw = (c_nw - m_n) * w_f, (c_sw - m_s) * w_f
+        c_ne, c_se = (c_ne - m_n) * e_f, (c_se - m_s) * e_f
 
         def row_smooth(x, lo, hi):
             left = jnp.where(trow == 0, lo, pltpu.roll(x, 1, 0))
             right = jnp.where(trow == tj - 1, hi, pltpu.roll(x, tj - 1, 0))
             return x + 0.25 * (left + right)
-        s_n = row_smooth(c_n, c_halo[o_nw:o_nw + 1], c_halo[o_ne:o_ne + 1])
-        s_s = row_smooth(c_s, c_halo[o_sw:o_sw + 1], c_halo[o_se:o_se + 1])
+        s_n, s_s = row_smooth(c_n, c_nw, c_ne), row_smooth(c_s, c_sw, c_se)
         s_w = c_w1 + 0.25 * (c_w2 + own_w - m_c)
         s_e = c_e1 + 0.25 * (own_e - m_c + c_e2)
         s_own = cbuf[...] - inner * spread(m_c)
@@ -408,7 +420,7 @@
         p = s_own * cext[0:elems]
         pbuf[g] = p
         s_rim = jnp.concatenate([s_n, s_s, s_w, s_e], axis=0)
-        p_rim = jnp.where(ok_rim, s_rim * cext[elems:elems + h], 0.0)
+        p_rim = s_rim * cext[elems:elems + h]
 
         hi, lo = cut(p)
         coef = fdot(jnp.where(low, hi.astype(F32), lo.astype(F32)).astype(BF16), Q)
@@ -422,19 +434,16 @@
         lifted = fdot(jnp.concatenate(cols, axis=1), cwts[...])
 
         def rim_lift(f, at, one, two):
-            b = f_halo[at:at + 16].astype(BF16)
+            b = halos[g, at:at + one.shape[0]]
             return fdot(jnp.concatenate([b * one, b * two], axis=1), wts[2 * f * n:(2 * f + 2) * n])
         last = elems - tj
-        north = rim_lift(0, o_n, masks[0, 0:tj], masks[1, 0:tj])
-        south = rim_lift(1, o_s, masks[2, last:elems], masks[3, last:elems])
-        west = rim_lift(2, o_w, rims[0], rims[1])
-        east = rim_lift(3, o_e, rims[2], rims[3])
+        north = rim_lift(0, 0, masks[0, 0:tj], masks[1, 0:tj])
+        south = rim_lift(1, tj, masks[2, last:elems], masks[3, last:elems])
+        west = rim_lift(2, 2 * tj, rims[0], rims[1])
+        east = rim_lift(3, 2 * tj + ti, rims[2], rims[3])
         for q in range(ti):
             at = slice(q * tj, (q + 1) * tj)
-            x = jnp.concatenate(cut(coef[at] * own_block), axis=1)
-            w = wmat[q]
-            y = fdot(x, jnp.concatenate([w, w], axis=0))
-            y = y[:, 0:n] + y[:, n:2 * n] + lifted[at]
+            y = small_dot(coef[at] * own_block, wmat[q]) + lifted[at]
             if q == 0:
                 y = y + north
             if q == ti - 1:
@@ -460,7 +469,7 @@
     fix(0, *edges)
     fill_sends(1, wbuf)
     start_all(rim_copies(1))
-    sums[1, ny + gy] = packed_rowsum(wbuf[...])
+    fill_sums(1, wbuf)
     share_lines(1)
     w1 = wbuf[...].reshape(elems, n)
     fbuf[...] = w1
@@ -489,51 +498,43 @@
     broadcast()
     full(0, rhs2)
     full(1, fbuf[...])
+    for g in range(2):
+        line_wait(g, "send")
+    for g in range(3):
+        rim_wait(g, "send")
+    bc_wait("send")
     bc_wait("recv")
     Y = msgs[:, 0, :]
-    l_n1, l_p, l_n2, l_a, l_b, l_n3 = [Y[:, q:q + 1] for q in range(6)]
+    l_n1, l_p, l_n2, l_a, l_b, l_n3 = [Y] + [pltpu.roll(Y, n - q, 1) for q in range(1, 6)]
 
     def over(x):
         return jnp.sum(x, axis=0, keepdims=True)
-    len2 = over(l_n1)
-    start_len = jnp.sqrt(len2)
-    h11 = over(l_p * l_n1) / len2
+    per_len2 = 1.0 / over(l_n1)
+    h11 = over(l_p * l_n1) * per_len2
     dev = l_p - h11
     gap2 = over(dev * dev * l_n1 + l_n2)
-    gap_len = jnp.sqrt(gap2)
-    h21 = gap_len / start_len
+    per_gap2 = 1.0 / gap2
+    ratio = gap2 * per_len2
     e_one = l_a - h11 * l_p
     e_two = l_b - h11
-    t12 = over(e_one * l_n1) / len2
-    h12 = t12 * start_len / gap_len
-    h22 = over(dev * e_one * l_n1 + e_two * l_n2) / gap2
+    t12 = over(e_one * l_n1) * per_len2
+    h22 = over(dev * e_one * l_n1 + e_two * l_n2) * per_gap2
     g_one = e_one - t12 - h22 * dev
     g_two = e_two - h22
-    h32 = jnp.sqrt(over(g_one * g_one * l_n1 + g_two * g_two * l_n2 + l_n3)) / gap_len
-
-    first = jnp.sqrt(h11 * h11 + h21 * h21)
-    cos_one = h11 / first
-    sin_one = h21 / first
-    upper = cos_one * h12 + sin_one * h22
-    lower = -sin_one * h12 + cos_one * h22
-    second = jnp.sqrt(lower * lower + h32 * h32)
-    cos_two = lower / second
-    y2 = cos_two * (-sin_one * start_len) / second
-    y1 = (cos_one * start_len - upper * y2) / first
-    c2 = y2 / gap_len
-    c1 = y1 / start_len - c2 * h11
+    last2 = over(g_one * g_one * l_n1 + g_two * g_two * l_n2 + l_n3) * per_gap2
+    first2 = h11 * h11 + ratio
+    lower = h11 * h22 - t12
+    c2 = -lower / (lower * lower + last2 * first2)
+    c1 = (h11 - c2 * (h11 * t12 + ratio * h22)) / first2 - c2 * h11
+    h21 = jnp.sqrt(ratio)
+    h12, h32 = t12 / h21, jnp.sqrt(last2)
+    c1, c2, h11, h12, h21, h22, h32 = [v[:, 0:1] for v in (c1, c2, h11, h12, h21, h22, h32)]
     out[...] = (c1 * zbuf[0] + c2 * zbuf[1]).reshape(ti, tj, n)
     hr, hc = iota((2, 3), 1), iota((2, 3), 0)
     hess_out[...] = jnp.where(
         hr == 0, jnp.where(hc == 0, h11, h12),
         jnp.where(hr == 1, jnp.where(hc == 0, h21, h22), jnp.where(hc == 0, 0.0, h32)))
 
-    bc_wait("send")
-    for g in range(2):
-        line_wait(g, "send")
-    for g in range(3):
-        rim_wait(g, "send")
-
 
 def hand_on(sol_in, hess_in, sol_out, hess_out):
     sol_out[...] = sol_in[...]
@@ -548,7 +549,6 @@
         kc = basis.shape[1]
         cflat = jnp.transpose(cinv, (0, 2, 3, 1)).reshape(ti, kc * kc, tj)
         sflat = jnp.transpose(state, (0, 2, 1))
-        hrows = 2 * tj + 4 * ti + 32
         h = 2 * ti + 2 * tj
         vm = pl.BlockSpec(memory_space=pltpu.VMEM)
         hbm = pl.BlockSpec(memory_space=pltpu.HBM)
@@ -577,21 +577,21 @@
                 pltpu.VMEM((ti * tj, n), F32),
                 pltpu.VMEM((ti * tj, n), F32),
                 pltpu.VMEM((ti, tj, n), F32),
-                pltpu.VMEM((2, hrows, n), F32),
-                pltpu.VMEM((2, hrows, n), F32),
+                pltpu.VMEM((2, h, n), BF16),
+                pltpu.VMEM((2, h, n), BF16),
                 pltpu.VMEM((h, n), F32),
                 pltpu.VMEM((h, n), F32),
-                pltpu.VMEM((2, 3 * ny, 1, n), F32),
+                pltpu.VMEM((2, 3 * ny, 8, n), F32),
                 pltpu.VMEM((nx * ny, 1, n), F32),
                 pltpu.SemaphoreType.DMA((5,)),
-                pltpu.SemaphoreType.DMA((ti,)),
-                pltpu.SemaphoreType.DMA((3, 8)),
-                pltpu.SemaphoreType.DMA((3, 8)),
+                pltpu.SemaphoreType.DMA((-(-ti // max(1, ti // 4)),)),
+                pltpu.SemaphoreType.DMA((3, 4)),
+                pltpu.SemaphoreType.DMA((3, 4)),
                 pltpu.SemaphoreType.DMA((2, 3)),
                 pltpu.SemaphoreType.DMA((2, 3)),
                 pltpu.SemaphoreType.DMA((1,)),
                 pltpu.SemaphoreType.DMA((1,)),
-                pltpu.SemaphoreType.REGULAR((max(1, nx.bit_length()),)),
+                pltpu.SemaphoreType.REGULAR((max(1, (nx - 2).bit_length() - 1),)),
             ],
             compiler_params=pltpu.CompilerParams(collective_id=0, has_side_effects=True,
                                                  vmem_limit_bytes=30000 * 1024),

time: 23.9 us -> 21 us (0.88)
  Pallas kernels: 23.1 us -> 20.2 us
    pallas_call x1, Pallas kernels: 22.4 us -> 19.5 us  [body(): pl.pallas_call(functools.partial(kernel, nx, ny, ti, tj, n, kc), out_shap...]
where the time goes in v3:
time: 21 us; the launch traced here: 20.8 us
  Pallas kernels  20.2 us (96%)
  between operations  0.64 us (3%)
    pallas_call x1, Pallas kernels, body(): pl.pallas_call(functools.partial(kernel, nx, ny, ti, tj, n, kc), out_shap...  19.5 us
    pallas_call x1, Pallas kernels, body(): pl.pallas_call(hand_on, out_shape=(jax.ShapeDtypeStruct(sol.shape, F32),...  0.67 us

profile of v3, /device:TPU:0, one launch (start us, length us, event | category | flops | bytes accessed | tf_op | source)
XLA Modules:
  0.0 20.8 jit_solution(11322342786247916527)
XLA Ops:
  0.6 19.5 %shard_map.77 = (f32[16,16,128]{2,1,0:T(8,128)S(1)}, f32[2,3]{1,0:T(2,128)S(1)}) custom-call(f32[16,16,128]{2,1,0:T(8,128)} %rhs_h.1, bf16[16,16,128,128]{3,2,1,0:T(8,128)(2,1)} %diag.1, bf16[4,128,128]{2,1,0:T(8,128)(2,1)} %lift_h.1, s32[16,4,16]{2,1,0:T(4,128)} %bitcast.7, f32[8,128]{1,0:T(8,128)} %bitcast.8, f32[16,64,16]{2,1,0:T(8,128)} %bitcast.6), custom_call_target="tpu_custom_call" | custom-call | tf_op jit(solution)/shard_map/pallas_call | solution.py:555
  20.1 0.7 %shard_map.78 = (f32[16,16,128]{2,1,0:T(8,128)}, f32[2,3]{1,0:T(2,128)}) custom-call(f32[16,16,128]{2,1,0:T(8,128)S(1)} %get-tuple-element.6.sol_in, f32[2,3]{1,0:T(2,128)S(1)} %get-tuple-element.7.hess_in), custom_call_target="tpu_custom_call" | custom-call | tf_op jit(solution)/shard_map/pallas_call | solution.py:599

commit v4 on v3

--- a/solution.py
+++ b/solution.py
@@ -72,8 +72,9 @@
 
     has_n, has_s, has_w, has_e = gx > 0, gx < nx - 1, gy > 0, gy < ny - 1
     n_i, s_i, w_i, e_i = [v.astype(jnp.int32) for v in (has_n, has_s, has_w, has_e)]
-    near = [(has_s, 1, k) for k in range(ny)] + [(None, 0, k) for k in range(1, ny)] + [
-        (has_n, -1, k) for k in range(ny)]
+    turns = list(range(1, ny))
+    near = [(has_s, 1, k) for k in turns[::-1] + [0]] + [(None, 0, k) for k in turns[::-1]] + [
+        (has_n, -1, k) for k in turns[::-1] + [0]]
     near_count = ny - 1 + ny * (n_i + s_i)
 
     def when(ok, run):
@@ -85,7 +86,7 @@
     sums[...] = jnp.zeros_like(sums)
     halos[...] = jnp.zeros_like(halos)
     chalo[...] = jnp.zeros_like(chalo)
-    for ok, d, k in near:
+    for ok, d, k in [(has_n, -1, k) for k in turns + [0]] + near[:2 * ny - 1]:
         def hello(d=d, k=k):
             pl.semaphore_signal(barrier, inc=1, device_id=(gx + d, lax.rem(gy + k, ny)), device_id_type=MESH)
         when(ok, hello)
@@ -98,6 +99,7 @@
     dcopies = [pltpu.make_async_copy(diag.at[pl.ds(q, group)], dvm.at[pl.ds(q, group)], dsem.at[q // group])
                for q in range(0, ti, group)]
     dcopies[0].start()
+    dcopies[1].start()
 
     steps = []
     r = 2
@@ -261,11 +263,11 @@
     csend[2 * tj + ti:2 * tj + 2 * ti] = c3d[:, tj - 1, :]
 
     pl.semaphore_wait(barrier, near_count)
+    share_lines(0)
     start_all(rim_copies(0))
-    share_lines(0)
     start_all(coarse_copies())
 
-    for c in dcopies[1:]:
+    for c in dcopies[2:]:
         c.start()
     RE = stacked(*spreads(row_k))
     row_le = one_hot(row_l)
@@ -273,7 +275,8 @@
     low_row = iota((n, n), 0) < kk
     RF = jnp.concatenate([RFh, jnp.where(low_row, RFl.astype(F32), 0.0).astype(BF16)], axis=0)
     G = one_hot(lax.rem(iota((n, n), 0), kc) == lax.rem(iota((n, n), 1), kk) // kc)
-    Q = one_hot(lax.rem(iota((n, n), 0), kc) == lax.rem(iota((n, n), 1), kc))
+    Q = one_hot(jnp.logical_and(low_row, lax.rem(iota((n, n), 0), kc) == lax.rem(iota((n, n), 1), kc)))
+    Q = jnp.concatenate([Q, Q], axis=0)
     flip = one_hot(iota((n, n), 0) + iota((n, n), 1) == n - 1)
     RR = jnp.concatenate([RFh, RFl], axis=1)
     loads[4].wait()
@@ -294,7 +297,7 @@
         col = fdot(jnp.where(own_j, wide, 0.0).astype(BF16), ones)
         masks[2 * f] = one_hot(col == 1.0)
         masks[2 * f + 1] = one_hot(col == 2.0)
-        packs[f] = (col == jnp.where(low, 1.0, 2.0)).astype(F32)
+        packs[f] = one_hot(col == jnp.where(low, 1.0, 2.0))
         if f >= 2:
             edge = col.reshape(ti, tj, n)[:, 0 if f == 2 else tj - 1, :]
             rims[2 * f - 4] = one_hot(edge == 1.0)
@@ -303,7 +306,9 @@
     jrow = lax.rem(iota((elems, 1), 0), tj)
     trow = iota((tj, 1), 0)
     scale = 1.0 / (ny * tj)
-    inner = 1.0 + 0.25 * ((jrow > 0).astype(F32) + (jrow < tj - 1).astype(F32))
+    irow = iota((1, 8, 1), 1)
+    inner_parts = [1.0 + 0.25 * ((irow + q * 8 > 0).astype(F32) + (irow + q * 8 < tj - 1).astype(F32))
+                   for q in range(tj // 8)]
 
     def spread(col):
         return jnp.broadcast_to(col[:, None, :], (ti, tj, n)).reshape(elems, n)
@@ -329,7 +334,7 @@
     none = jnp.zeros((kc, n), BF16)
     coarse_rows = jnp.concatenate([
         jnp.concatenate([Rh, none], axis=1), jnp.concatenate([none, Rh], axis=1)], axis=0)
-    own_block = (iota((tj, n), 1) // kc == iota((tj, n), 0)).astype(F32)
+    own_block = one_hot(iota((tj, n), 1) // kc == iota((tj, n), 0))
 
     def local_lifts(x):
         b = x.astype(BF16)
@@ -395,6 +400,14 @@
             lanes(part_of(g, 0, 1, 1), pick), lanes(part_of(g, 0, 1, 2), pick),
             lanes(part_of(g, -1, 0, 6), pick_j), lanes(part_of(g, 1, 0, 5), pick_j), singles], axis=0)
         wide = exact_dot(stack, G)
+        def rim_lift(f, at, one, two):
+            b = halos[g, at:at + one.shape[0]]
+            return fdot(jnp.concatenate([b * one, b * two], axis=1), wts[2 * f * n:(2 * f + 2) * n])
+        last = elems - tj
+        north = rim_lift(0, 0, masks[0, 0:tj], masks[1, 0:tj])
+        south = rim_lift(1, tj, masks[2, last:elems], masks[3, last:elems])
+        west = rim_lift(2, 2 * tj, rims[0], rims[1])
+        east = rim_lift(3, 2 * tj + ti, rims[2], rims[3])
         m_c, c_w1, c_w2, c_e1, c_e2 = [wide[q * ti:(q + 1) * ti] for q in range(5)]
         c_n, c_s = wide[5 * ti:5 * ti + tj], wide[5 * ti + tj:5 * ti + 2 * tj]
         one = wide[5 * ti + 2 * tj:]
@@ -414,42 +427,57 @@
         s_n, s_s = row_smooth(c_n, c_nw, c_ne), row_smooth(c_s, c_sw, c_se)
         s_w = c_w1 + 0.25 * (c_w2 + own_w - m_c)
         s_e = c_e1 + 0.25 * (own_e - m_c + c_e2)
-        s_own = cbuf[...] - inner * spread(m_c)
-        s_own = s_own + jnp.where(jrow == 0, spread(0.25 * c_w1), 0.0) + jnp.where(
-            jrow == tj - 1, spread(0.25 * c_e1), 0.0)
-        p = s_own * cext[0:elems]
-        pbuf[g] = p
+        sub = iota((1, 8, 1), 1)
+        parts = tj // 8
+
+        def groups(x):
+            return [x.reshape(ti, parts, 8, n)[:, q] for q in range(parts)]
+
+        def whole(xs):
+            return jnp.concatenate([x[:, None] for x in xs], axis=1).reshape(elems, n)
+
+        def tall(x):
+            return jnp.broadcast_to(x[:, None, :], (ti, 8, n))
+        m_t, w_t, e_t = tall(m_c), tall(c_w1), tall(c_e1)
+        first_w = jnp.where(sub == 0, 0.25, 0.0)
+        last_e = jnp.where(sub == 7, 0.25, 0.0)
+        p_parts = []
+        for q, (c, k) in enumerate(zip(groups(cbuf[...]), groups(cext[0:elems]))):
+            x = c - inner_parts[q] * m_t
+            if q == 0:
+                x = x + first_w * w_t
+            if q == parts - 1:
+                x = x + last_e * e_t
+            p_parts.append(x * k)
         s_rim = jnp.concatenate([s_n, s_s, s_w, s_e], axis=0)
         p_rim = s_rim * cext[elems:elems + h]
-
+        p = whole(p_parts)
+        pbuf[g] = p
         hi, lo = cut(p)
-        coef = fdot(jnp.where(low, hi.astype(F32), lo.astype(F32)).astype(BF16), Q)
+        coef = fdot(jnp.concatenate([hi, lo], axis=1), Q)
+        rim_w, rim_e = tall(p_rim[2 * tj:2 * tj + ti]), tall(p_rim[2 * tj + ti:2 * tj + 2 * ti])
+        down = [pltpu.roll(x, 1, 1) for x in p_parts]
+        up = [pltpu.roll(x, 7, 1) for x in p_parts]
+        left = [jnp.where(sub == 0, rim_w if q == 0 else down[q - 1], down[q]) for q in range(parts)]
+        right = [jnp.where(sub == 7, rim_e if q == parts - 1 else up[q + 1], up[q]) for q in range(parts)]
+        rim_h = p_rim[0:2 * tj].astype(BF16)
         nb = [
-            jnp.concatenate([p_rim[0:tj], p[0:elems - tj]], axis=0),
-            jnp.concatenate([p[tj:], p_rim[tj:2 * tj]], axis=0),
-            left_of(p, spread(p_rim[2 * tj:2 * tj + ti])),
-            right_of(p, spread(p_rim[2 * tj + ti:2 * tj + 2 * ti])),
+            jnp.concatenate([rim_h[0:tj], hi[0:elems - tj]], axis=0),
+            jnp.concatenate([hi[tj:], rim_h[tj:2 * tj]], axis=0),
+            whole(left).astype(BF16),
+            whole(right).astype(BF16),
         ]
-        cols = [(nb[f] * packs[f]).astype(BF16) for f in range(4)]
-        lifted = fdot(jnp.concatenate(cols, axis=1), cwts[...])
-
-        def rim_lift(f, at, one, two):
-            b = halos[g, at:at + one.shape[0]]
-            return fdot(jnp.concatenate([b * one, b * two], axis=1), wts[2 * f * n:(2 * f + 2) * n])
-        last = elems - tj
-        north = rim_lift(0, 0, masks[0, 0:tj], masks[1, 0:tj])
-        south = rim_lift(1, tj, masks[2, last:elems], masks[3, last:elems])
-        west = rim_lift(2, 2 * tj, rims[0], rims[1])
-        east = rim_lift(3, 2 * tj + ti, rims[2], rims[3])
+        lifted = fdot(jnp.concatenate([nb[f] * packs[f] for f in range(4)], axis=1), cwts[...])
+        c_hi, c_lo = cut(coef)
+        base = []
+        for q in range(ti):
+            side = jnp.where(trow == 0, west[q:q + 1], jnp.where(trow == tj - 1, east[q:q + 1], 0.0))
+            x = wbuf[q] + lifted[q * tj:(q + 1) * tj] + side
+            base.append(x + north if q == 0 else x + south if q == ti - 1 else x)
         for q in range(ti):
             at = slice(q * tj, (q + 1) * tj)
-            y = small_dot(coef[at] * own_block, wmat[q]) + lifted[at]
-            if q == 0:
-                y = y + north
-            if q == ti - 1:
-                y = y + south
-            side = jnp.where(trow == 0, west[q:q + 1], jnp.where(trow == tj - 1, east[q:q + 1], 0.0))
-            wbuf[q] += y + side
+            y = fdot(jnp.concatenate([c_hi[at] * own_block, c_lo[at] * own_block], axis=0), wmat[q])
+            wbuf[q] = base[q] + y[0:tj, 0:n] + (y[tj:2 * tj, 0:n] + y[0:tj, n:2 * n])
 
     def full(g, x):
         hi, lo = cut(pbuf[g])
@@ -568,7 +596,7 @@
                 pltpu.VMEM((4 * n, n), BF16),
                 pltpu.VMEM((ti, tj * kc, 2 * n), BF16),
                 pltpu.VMEM((8, ti * tj, n), BF16),
-                pltpu.VMEM((4, ti * tj, n), F32),
+                pltpu.VMEM((4, ti * tj, n), BF16),
                 pltpu.VMEM((4, ti, n), BF16),
                 pltpu.VMEM((ti * tj + h, n), F32),
                 pltpu.VMEM((2, ti * tj, n), F32),

time: 21 us -> 20.5 us (0.976)
  Pallas kernels: 20.2 us -> 19.7 us
    pallas_call x1, Pallas kernels: 19.5 us -> 19.1 us  [body(): pl.pallas_call(functools.partial(kernel, nx, ny, ti, tj, n, kc), out_shap...]
where the time goes in v4:
time: 20.5 us; the launch traced here: 20.4 us
  Pallas kernels  19.7 us (96%)
  between operations  0.64 us (3%)
    pallas_call x1, Pallas kernels, body(): pl.pallas_call(functools.partial(kernel, nx, ny, ti, tj, n, kc), out_shap...  19.1 us
    pallas_call x1, Pallas kernels, body(): pl.pallas_call(hand_on, out_shape=(jax.ShapeDtypeStruct(sol.shape, F32),...  0.67 us

profile of v4, /device:TPU:0, one launch (start us, length us, event | category | flops | bytes accessed | tf_op | source)
XLA Modules:
  0.0 20.4 jit_solution(9256124839146480915)
XLA Ops:
  0.6 19.1 %shard_map.77 = (f32[16,16,128]{2,1,0:T(8,128)S(1)}, f32[2,3]{1,0:T(2,128)S(1)}) custom-call(f32[16,16,128]{2,1,0:T(8,128)} %rhs_h.1, bf16[16,16,128,128]{3,2,1,0:T(8,128)(2,1)} %diag.1, bf16[4,128,128]{2,1,0:T(8,128)(2,1)} %lift_h.1, s32[16,4,16]{2,1,0:T(4,128)} %bitcast.7, f32[8,128]{1,0:T(8,128)} %bitcast.8, f32[16,64,16]{2,1,0:T(8,128)} %bitcast.6), custom_call_target="tpu_custom_call" | custom-call | tf_op jit(solution)/shard_map/pallas_call | solution.py:583
  19.7 0.7 %shard_map.78 = (f32[16,16,128]{2,1,0:T(8,128)}, f32[2,3]{1,0:T(2,128)}) custom-call(f32[16,16,128]{2,1,0:T(8,128)S(1)} %get-tuple-element.6.sol_in, f32[2,3]{1,0:T(2,128)S(1)} %get-tuple-element.7.hess_in), custom_call_target="tpu_custom_call" | custom-call | tf_op jit(solution)/shard_map/pallas_call | solution.py:627

commit v5 on v4

--- a/solution.py
+++ b/solution.py
@@ -122,7 +122,7 @@
     def line_copy(g, d, k):
         return pltpu.make_async_remote_copy(
             src_ref=sums.at[g, ny + gy], dst_ref=sums.at[g, (1 - d) * ny + gy],
-            send_sem=lsend.at[g, d + 1], recv_sem=lrecv.at[g, 1 - d],
+            send_sem=lsend.at[g], recv_sem=lrecv.at[g],
             device_id=(gx + d, lax.rem(gy + k, ny)), device_id_type=MESH)
 
     def share_lines(g):
@@ -130,17 +130,19 @@
             when(ok, lambda d=d, k=k: line_copy(g, d, k).start())
 
     def line_wait(g, which):
-        for ok, d in ((has_n, -1), (has_s, 1), (None, 0)):
-            def one(d=d):
-                part = sums.at[g, pl.ds((d + 1) * ny, ny if d else ny - 1)]
-                c = pltpu.make_async_remote_copy(
-                    src_ref=part, dst_ref=part, send_sem=lsend.at[g, d + 1], recv_sem=lrecv.at[g, d + 1],
-                    device_id=(gx, gy), device_id_type=MESH)
-                if which == "send":
-                    c.wait_send()
-                else:
-                    c.wait_recv()
-            when(ok, one)
+        for lines in range(3):
+            messages = ny * (lines + 1) - 1
+            if messages:
+                @pl.when(n_i + s_i == lines)
+                def _(messages=messages):
+                    part = sums.at[g, pl.ds(0, messages)]
+                    c = pltpu.make_async_remote_copy(
+                        src_ref=part, dst_ref=part, send_sem=lsend.at[g], recv_sem=lrecv.at[g],
+                        device_id=(gx, gy), device_id_type=MESH)
+                    if which == "send":
+                        c.wait_send()
+                    else:
+                        c.wait_recv()
 
     h = 2 * ti + 2 * tj
     croutes = [
@@ -519,10 +521,10 @@
     fix(1, *edges)
     w2 = wbuf[...].reshape(elems, n)
     rhs2, gap = rhs[...].reshape(elems, n), gbuf[...]
-    p_two = safe_div(total(rhs2 * w2), own_n1)
-    q_two = safe_div(total(gap * w2), own_n2)
-    rest = w2 - p_two * rhs2 - q_two * gap
-    msgs[me] = message([own_n1, p_one, own_n2, p_two, q_two, total(rest * rest)])
+    on_rhs, on_gap, square = total(rhs2 * w2), total(gap * w2), total(w2 * w2)
+    p_two, q_two = safe_div(on_rhs, own_n1), safe_div(on_gap, own_n2)
+    rest = jnp.maximum(square - p_two * on_rhs - q_two * on_gap, 0.0)
+    msgs[me] = message([own_n1, p_one, own_n2, p_two, q_two, rest])
     broadcast()
     full(0, rhs2)
     full(1, fbuf[...])
@@ -564,9 +566,12 @@
         jnp.where(hr == 1, jnp.where(hc == 0, h21, h22), jnp.where(hc == 0, 0.0, h32)))
 
 
-def hand_on(sol_in, hess_in, sol_out, hess_out):
-    sol_out[...] = sol_in[...]
-    hess_out[...] = hess_in[...]
+def hand_on(sol_in, hess_in, sol_out, hess_out, sem):
+    copies = [pltpu.make_async_copy(sol_in, sol_out, sem.at[0]), pltpu.make_async_copy(hess_in, hess_out, sem.at[1])]
+    for c in copies:
+        c.start()
+    for c in copies:
+        c.wait()
 
 
 def solution(mesh):
@@ -615,8 +620,8 @@
                 pltpu.SemaphoreType.DMA((-(-ti // max(1, ti // 4)),)),
                 pltpu.SemaphoreType.DMA((3, 4)),
                 pltpu.SemaphoreType.DMA((3, 4)),
-                pltpu.SemaphoreType.DMA((2, 3)),
-                pltpu.SemaphoreType.DMA((2, 3)),
+                pltpu.SemaphoreType.DMA((2,)),
+                pltpu.SemaphoreType.DMA((2,)),
                 pltpu.SemaphoreType.DMA((1,)),
                 pltpu.SemaphoreType.DMA((1,)),
                 pltpu.SemaphoreType.REGULAR((max(1, (nx - 2).bit_length() - 1),)),
@@ -628,7 +633,8 @@
             hand_on,
             out_shape=(jax.ShapeDtypeStruct(sol.shape, F32), jax.ShapeDtypeStruct(hess.shape, F32)),
             in_specs=[vm, vm],
-            out_specs=(vm, vm),
+            out_specs=(hbm, hbm),
+            scratch_shapes=[pltpu.SemaphoreType.DMA((2,))],
             compiler_params=pltpu.CompilerParams(vmem_limit_bytes=30000 * 1024),
         )(sol, hess)
         return sol, hess.T

time: 20.5 us -> 20.3 us (level)
  no operation moved by 1% of the time
where the time goes in v5:
time: 20.3 us; the launch traced here: 20.2 us
  Pallas kernels  19.6 us (97%)
  between operations  0.64 us (3%)
    pallas_call x1, Pallas kernels, body(): pl.pallas_call(functools.partial(kernel, nx, ny, ti, tj, n, kc), out_shap...  18.9 us
    pallas_call x1, Pallas kernels, body(): pl.pallas_call(hand_on, out_shape=(jax.ShapeDtypeStruct(sol.shape, F32),...  0.68 us

profile of v5, /device:TPU:0, one launch (start us, length us, event | category | flops | bytes accessed | tf_op | source)
XLA Modules:
  0.0 20.2 jit_solution(2587491035106525548)
XLA Ops:
  0.6 18.9 %shard_map.77 = (f32[16,16,128]{2,1,0:T(8,128)S(1)}, f32[2,3]{1,0:T(2,128)S(1)}) custom-call(f32[16,16,128]{2,1,0:T(8,128)} %rhs_h.1, bf16[16,16,128,128]{3,2,1,0:T(8,128)(2,1)} %diag.1, bf16[4,128,128]{2,1,0:T(8,128)(2,1)} %lift_h.1, s32[16,4,16]{2,1,0:T(4,128)} %bitcast.7, f32[8,128]{1,0:T(8,128)} %bitcast.8, f32[16,64,16]{2,1,0:T(8,128)} %bitcast.6), custom_call_target="tpu_custom_call" | custom-call | tf_op jit(solution)/shard_map/pallas_call | solution.py:588
  19.5 0.7 %shard_map.78 = (f32[16,16,128]{2,1,0:T(8,128)}, f32[2,3]{1,0:T(2,128)}) custom-call(f32[16,16,128]{2,1,0:T(8,128)S(1)} %get-tuple-element.6.sol_in, f32[2,3]{1,0:T(2,128)S(1)} %get-tuple-element.7.hess_in), custom_call_target="tpu_custom_call" | custom-call | tf_op jit(solution)/shard_map/pallas_call | solution.py:632
